TPU v7x, 32 devices: a whole 2x2x4 slice. The times are simulated.
32 devices in a mesh: dp: 8 (over y, x, core), tp: 4 (over z).
Axes of the slice: x: 2, y: 2, z: 4, core: 2. Of those that a mesh axis runs over, the one named last changes fastest.
Arguments:
- hidden: bfloat16 [32, 512, 1024], P(('dp', 'tp')), may hold values from -6 to 6
- cell_ids: int32 [32, 512], P(('dp', 'tp')), may hold values from 0 to 63, never falling along the last dimension, each value on 1 to 60 neighbouring positions
- cell_boxes: int32 [32, 64, 4], P(('dp', 'tp')), may hold values from 0 to 1000
- cotangent: bfloat16 [32, 512, 1024], P(('dp', 'tp')), may hold values from -6 to 6
- weight_cols: bfloat16 [7, 1024, 1024], P(None, None, 'tp'), may hold values from -0.1875 to 0.1875
- weight_out: bfloat16 [1024, 1024], P('tp'), may hold values from -1.5 to 1.5
- weight_down: bfloat16 [4, 1024, 1024], P(None, 'tp'), may hold values from -0.09375 to 0.09375
- vectors: float32 [1024, 12], replicated
- vector_moment: float32 [1024, 12], P('dp')
- left_stat: float32 [16, 1024, 1024], P('dp', 'tp')
- right_stat: float32 [16, 1024, 1024], P('dp', 'tp')
- left_root: float32 [16, 1024, 1024], P('dp', 'tp')
- right_root: float32 [16, 1024, 1024], P('dp')
- master: float32 [16, 1024, 1024], P('dp', 'tp'), may hold values from -0.1875 to 0.1875
- averaged_weight: float32 [16, 1024, 1024], P('dp', 'tp'), may hold values from -0.1875 to 0.1875
Outputs:
- layer_out: float32 [32, 512, 1024], P(('dp', 'tp'))
- input_grad: float32 [32, 512, 1024], P(('dp', 'tp'))
- block_grad: float32 [16, 1024, 1024], P('dp', None, 'tp')
- left_new: float32 [16, 1024, 1024], P('dp', 'tp')
- right_new: float32 [16, 1024, 1024], P('dp', 'tp')
- master_new: float32 [16, 1024, 1024], P('dp', 'tp')
- weight_copy: bfloat16 [16, 1024, 1024], P('dp', 'tp')
- ema_new: float32 [16, 1024, 1024], P('dp', 'tp')
- vector_grad: float32 [1024, 12], P('dp')
- moment_new: float32 [1024, 12], P('dp')
- vector_new: float32 [1024, 12], P('dp')
- bias_grad: float32 [1024], P('dp')
Inputs may be any that keep to these rules, and one draw needn't show every extreme that they name: `cell_ids`: on each page cell numbers never fall; each cell spans 1 to 60 consecutive tokens and some cell exactly 60.
All inputs are finite; a program needn't handle non-finite values.
Results may differ from a plain program's by a relative error of at most 0.022.
The roundings to bfloat16 on the way count: a program that leaves them out, or rounds other values in their place, can miss the bound.
Values may be sent and summed in bfloat16 or wider, within the bound.
A program may use at most 256 MiB of HBM per device.

v0:
```python
import math

import jax
import jax.numpy as jnp
from jax import lax
from jax.experimental import pallas as pl
from jax.experimental.pallas import tpu as pltpu
from jax.sharding import PartitionSpec as P

MODEL_WIDTH = 1024
H = 16
HD = 64

PRECISE = lax.Precision.HIGHEST
EPS_NORM = 1e-06
STAT_DECAY = 0.5
BLOCK_RATE = 0.7
EMA_DECAY = 0.9
MOMENTUM = 0.9
VEC_RATE = 0.2

MESH = pl.DeviceIdType.MESH


def position():
    d, z = lax.axis_index("dp"), lax.axis_index("tp")
    core, x, y = d % 2, (d // 2) % 2, d // 4
    near = {
        "x": (d + 2 - 4 * x, z),
        "y": (d + 4 - 8 * y, z),
        "c": (d + 1 - 2 * core, z),
        "u": (d, z + 1),
        "v": (d, z - 1),
    }
    return z, core, x, y, near


def meet(z, near, extra=()):
    barrier = pltpu.get_barrier_semaphore()
    always = [near[name] for name in "xyc"] + list(extra)
    for device in always:
        pl.semaphore_signal(barrier, 1, device_id=device, device_id_type=MESH)

    @pl.when(z < 3)
    def _():
        pl.semaphore_signal(barrier, 1, device_id=near["u"], device_id_type=MESH)

    @pl.when(z > 0)
    def _():
        pl.semaphore_signal(barrier, 1, device_id=near["v"], device_id_type=MESH)

    pl.semaphore_wait(barrier, len(always) + (z + 2) // 3 + (5 - z) // 3)


ORDER = (0, 1, 2, 7, 3, 4, 5, 6, 8, 9, 10, 11)


NT = (((1,), (1,)), ((), ()))
TOKENS = 512
WIDE = MODEL_WIDTH


def dot(a, b):
    return jnp.dot(a, b, preferred_element_type=jnp.float32)


def dot_nt(a, b):
    return lax.dot_general(a, b, NT, preferred_element_type=jnp.float32)


def columns(i, width=256):
    return pl.ds(pl.multiple_of(i * width, width), width)


def loop(count, body):
    def step(i, carry):
        body(i)
        return carry

    lax.fori_loop(0, count, step, 0)


def mean_of(rows):
    return jnp.sum(rows, -1, keepdims=True) * (1.0 / WIDE)


def transpose_into(dest, source):
    def body(i):
        dest[columns(i), :] = source[:, columns(i)].T

    loop(WIDE // 256, body)


def transpose_back(dest, source):
    def body(i):
        dest[:, columns(i)] = source[columns(i), :].T

    loop(WIDE // 256, body)


def embed_tokens(hidden, ids, boxes, x_ref, x_low):
    cells = boxes.shape[0]
    half = WIDE // 8
    place = lax.broadcasted_iota(jnp.int32, (1, half), 1).astype(jnp.float32)
    rate = jnp.exp(place * (-math.log(1000.0) / half))
    marks = lax.broadcasted_iota(jnp.int32, (cells, TOKENS), 0) == ids[...]
    chosen = jnp.where(marks, 1.0, 0.0).T.astype(jnp.bfloat16)
    for c in range(4):
        angle = boxes[:, c : c + 1].astype(jnp.float32) * rate
        for kind, wave in enumerate((jnp.sin(angle), jnp.cos(angle))):
            wave = 0.5 * wave
            high = wave.astype(jnp.bfloat16)
            rest = wave - high.astype(jnp.float32)
            middle = rest.astype(jnp.bfloat16)
            low = (rest - middle.astype(jnp.float32)).astype(jnp.bfloat16)
            emb = dot(chosen, high) + (dot(chosen, middle) + dot(chosen, low))
            at = pl.ds(c * 2 * half + kind * half, half)
            value = hidden[:, at].astype(jnp.float32) + emb
            x_ref[:, at] = value
            x_low[:, at] = value.astype(jnp.bfloat16)


def project(x_low, weight, dest, bias, scale):
    def body(i):
        value = dot(x_low[...], weight[:, columns(i)])
        if bias is not None:
            value = value + bias[:, columns(i)]
        value = value.astype(jnp.bfloat16)
        if scale:
            value = value * jnp.asarray(HD ** (-0.5), jnp.bfloat16)
        dest[:, columns(i)] = value

    loop(WIDE // 256, body)


def half_mask(e, shape):
    lane = lax.broadcasted_iota(jnp.int32, shape, 1)
    return (lane < HD) if e == 0 else (lane >= HD)


def attend_pair(t, q8, k, v_t, ctx_t, stat):
    at = columns(t, 128)
    keys, queries = k[:, at], q8[:, at]
    for e in range(2):
        own = jnp.where(half_mask(e, queries.shape), queries, jnp.zeros_like(queries))
        scores = dot_nt(keys, own)
        top = jnp.max(scores, 0, keepdims=True)
        power = jnp.exp(scores - top)
        total = jnp.sum(power, 0, keepdims=True)
        probs = (power * (1.0 / total)).astype(jnp.bfloat16)
        rows = pl.ds(pl.multiple_of(t * 128 + e * 64, 64), 64)
        ctx_t[rows, :] = dot(v_t[rows, :], probs).astype(jnp.bfloat16)
        stat[2 * t + e, :, :] = top + jnp.log(total)


def norm_rows(values, gain, shift):
    center = values - mean_of(values)
    inv = lax.rsqrt(mean_of(center * center) + EPS_NORM)
    normed = center * inv
    return normed * gain + shift, normed, inv


SLICE = 64


def row_loop(body):
    loop(TOKENS // SLICE, lambda i: body(pl.ds(pl.multiple_of(i * SLICE, SLICE), SLICE)))


def gelu_both(value):
    phi = 0.5 * (1.0 + lax.erf(value * math.sqrt(0.5)))
    density = jnp.exp(-0.5 * value * value) * (1.0 / math.sqrt(2.0 * math.pi))
    return value * phi, phi + value * density


def forward_kernel(
    cols, outw, down, hidden, ids, boxes, cotangent, vec,
    full_out, layer_out, x_out, q_out, k_out, kt_out, v_out, ctx_out, stat_out, mid_out, hat_out, inv_out, act_out, slope_out,
    two_out, sums_out,
    w, x_t, mid_t, k_t, x_ref, x_low, q8, k, v, v_t, ctx_t, ctx, stat, acc, mid, mid_low, hat, inv, act, slope, y_out, two, sums,
    load, along, onward, arrived, beside, store, spill,
):
    z, core, x, y, near = position()
    p = 2 * y + x
    meet(z, near)

    def own(kk, h):
        if kk < 7:
            return cols.at[kk, pl.ds(h * 512, 512), :]
        if kk == 7:
            return outw.at[pl.ds(h * 128, 128), :]
        return down.at[kk - 8, pl.ds(h * 128, 128), :]

    def spot(s, kk, h):
        if kk < 7:
            return w.at[kk, pl.ds(h * 512, 512), pl.ds(pl.multiple_of(s * 256, 256), 256)]
        return w.at[kk, pl.ds(pl.multiple_of(s * 256 + h * 128, 128), 128), :]

    def spot_whole(s, kk):
        if kk < 7:
            return w.at[kk, :, pl.ds(pl.multiple_of(s * 256, 256), 256)]
        return w.at[kk, pl.ds(pl.multiple_of(s * 256, 256), 256), :]

    def whole_own(kk):
        if kk < 7:
            return cols.at[kk]
        return outw if kk == 7 else down.at[kk - 8]

    def to(source, s, kk, send_sem, recv_sem, name):
        return pltpu.make_async_remote_copy(
            src_ref=source,
            dst_ref=spot(s, kk, core),
            send_sem=send_sem,
            recv_sem=recv_sem.at[s, kk],
            device_id=near[name],
            device_id_type=MESH,
        )

    def first(g, act_on):
        for t in range(3):
            kk = ORDER[3 * g + t]
            mine = (p == t) | (p == 3) if t == 0 else p == t

            @pl.when(mine & (z < 3))
            def _(kk=kk):
                act_on(to(own(kk, core), z, kk, along.at[kk], arrived, "u"))

            @pl.when(mine & (z > 0))
            def _(kk=kk):
                act_on(to(own(kk, core), z, kk, onward.at[0, z, kk], arrived, "v"))

    far = 3 * (1 - z // 2)
    nearest = z + 1 - 2 * (z // 3)
    strips = (nearest, 6 - nearest - far - z, far)

    def item(n, t):
        return strips[n % 3], ORDER[3 * (n // 3) + t]

    def go(s, kk, kind, name, sems):
        return to(spot(s, kk, core), s, kk, onward.at[kind, s, kk], sems, name)

    def stage(n, hop, begin):
        for t in range(3):
            s, kk = item(n, t)
            who = {
                (0, 0): (p == 0) | (p == 3),
                (0, 1): p == 1,
                (0, 2): p == 2,
                (1, 0): (p == 1) | (p == 2),
                (1, 1): (p == 0) | (p == 3),
                (1, 2): (p == 0) | (p == 3),
                (2, 0): None,
                (2, 1): p == 2,
                (2, 2): p == 1,
            }[hop, t]
            if who is None:
                continue

            @pl.when(who)
            def _(s=s, kk=kk, t=t):
                if begin:
                    go(s, kk, 0, "x", arrived).wait_recv()

                def act_on(copy):
                    if begin:
                        copy.start()
                    else:
                        copy.wait_send()

                if hop == 0:

                    @pl.when((s > z) & (z > 0))
                    def _():
                        act_on(go(s, kk, 0, "v", arrived))

                    @pl.when((s < z) & (z < 3))
                    def _():
                        act_on(go(s, kk, 0, "u", arrived))

                    if t == 0:

                        @pl.when(p == 0)
                        def _():
                            act_on(go(s, kk, 1, "x", arrived))
                            act_on(go(s, kk, 2, "y", arrived))
                    else:
                        act_on(go(s, kk, 1, "x", arrived))
                        act_on(go(s, kk, 2, "y", arrived))
                if hop == 1 and t == 1:

                    @pl.when(p == 3)
                    def _():
                        act_on(go(s, kk, 1, "x", arrived))

                if hop == 1 and t == 2:

                    @pl.when(p == 3)
                    def _():
                        act_on(go(s, kk, 2, "y", arrived))

                act_on(go(s, kk, 3, "c", beside))

    copies = []

    def keep(source, dest):
        copy = pltpu.make_async_copy(source, dest, spill.at[len(copies)])
        copy.start()
        copies.append(copy)

    def ready(kk):
        pltpu.make_async_copy(whole_own(kk), spot_whole(z, kk), load.at[kk]).wait()
        for s in strips:
            pltpu.make_async_remote_copy(
                src_ref=spot(s, kk, 1 - core),
                dst_ref=spot(s, kk, 1 - core),
                send_sem=onward.at[3, s, kk],
                recv_sem=beside.at[s, kk],
                device_id=near["c"],
                device_id_type=MESH,
            ).wait_recv()
        copy = pltpu.make_async_copy(w.at[kk], full_out.at[kk], store.at[kk])
        copy.start()

    def unit_embed():
        embed_tokens(hidden, ids, boxes, x_ref, x_low)
        transpose_into(x_t, x_low)
        keep(x_t, x_out)

    def unit_qkv():
        for kk in range(3):
            ready(kk)
        project(x_low, w.at[0], q8, vec.at[6:7], True)
        project(x_low, w.at[1], k, None, False)
        project(x_low, w.at[2], v, vec.at[7:8], False)
        transpose_into(v_t, v)
        transpose_into(k_t, k)
        keep(q8, q_out)
        keep(k_t, kt_out)
        keep(k, k_out)
        keep(v, v_out)

    def unit_attend(lo, hi):
        loop(hi - lo, lambda i: attend_pair(lo + i, q8, k, v_t, ctx_t, stat))

    def unit_context():
        transpose_back(ctx, ctx_t)
        keep(ctx, ctx_out)
        keep(stat, stat_out)

    def unit_mid():
        ready(7)

        def tile(i):
            acc[:, columns(i)] = dot(ctx[...], w[7, :, columns(i)])

        loop(WIDE // 256, tile)

        def rows(r):
            value = x_ref[r, :] + acc[r, :] + vec[0:1, :]
            out, normed, scale = norm_rows(value, vec[2:3, :], vec[3:4, :])
            mid[r, :] = out
            mid_low[r, :] = out.astype(jnp.bfloat16)
            hat[r, :] = normed
            inv[r, :] = jnp.broadcast_to(scale, (SLICE, 128))

        row_loop(rows)
        transpose_into(mid_t, mid_low)
        keep(mid_t, mid_out)
        keep(hat, hat_out)
        keep(inv, inv_out)

    def unit_up(u):
        ready(3 + u)
        def tile(i):
            at = columns(i)
            slot = i % 2

            @pl.when(i >= 2)
            def _():
                pltpu.make_async_copy(slope.at[slot], slope_out.at[u, :, at], store.at[12 + slot]).wait()

            for part in range(2):
                rows = pl.ds(part * 256, 256)
                value = dot(mid_low[rows, :], w[3 + u, :, at]) + vec[8 + u : 9 + u, at]
                out, grad = gelu_both(value)
                act[u, rows, at] = out.astype(jnp.bfloat16)
                slope[slot, rows, :] = grad
            pltpu.make_async_copy(slope.at[slot], slope_out.at[u, :, at], store.at[12 + slot]).start()

        loop(WIDE // 256, tile)
        for slot in range(2):
            pltpu.make_async_copy(slope.at[slot], slope_out.at[u, :, columns(slot)], store.at[12 + slot]).wait()
        keep(act.at[u], act_out.at[u])

    def unit_down(u):
        ready(8 + u)

        def tile(i):
            at = columns(i)
            value = dot(act[u], w[8 + u, :, at])
            acc[:, at] = value if u == 0 else acc[:, at] + value

        loop(WIDE // 256, tile)

    def unit_last():
        sums[...] = jnp.zeros_like(sums)

        def rows(r):
            value = mid[r, :] + acc[r, :] + vec[1:2, :]
            out, normed, scale = norm_rows(value, vec[4:5, :], vec[5:6, :])
            y_out[r, :] = out
            grad = cotangent[r, :].astype(jnp.float32)
            scaled = grad * vec[4:5, :]
            arg = scale * (scaled - mean_of(scaled) - normed * mean_of(scaled * normed))
            two[r, :] = arg
            sums[1:2, :] += jnp.sum(arg, 0, keepdims=True)
            sums[4:5, :] += jnp.sum(grad * normed, 0, keepdims=True)
            sums[5:6, :] += jnp.sum(grad, 0, keepdims=True)

        row_loop(rows)
        keep(y_out, layer_out)
        keep(two, two_out)
        keep(sums, sums_out)

    first(0, lambda copy: copy.start())
    first(1, lambda copy: copy.start())
    for kk in ORDER:
        pltpu.make_async_copy(whole_own(kk), spot_whole(z, kk), load.at[kk]).start()
    unit_embed()
    after = {
        4: unit_qkv,
        5: lambda: unit_attend(0, 4),
        6: lambda: (unit_attend(4, 8), unit_context()),
        7: unit_mid,
        8: lambda: unit_up(0),
        9: lambda: unit_up(1),
        10: lambda: unit_up(2),
        11: lambda: unit_up(3),
        12: lambda: unit_down(0),
        13: lambda: (unit_down(1), unit_down(2), unit_down(3), unit_last()),
    }
    for n in range(14):
        if n in (3, 6):
            first(n // 3 + 1, lambda copy: copy.start())
        for hop in range(3):
            if 0 <= n - hop < 12:
                stage(n - hop, hop, True)
        if n in after:
            after[n]()
    for n in range(12):
        for hop in range(3):
            stage(n, hop, False)
    for g in range(4):
        first(g, lambda copy: copy.wait_send())
    for kk in ORDER:
        pltpu.make_async_copy(w.at[kk], full_out.at[kk], store.at[kk]).wait()
    for copy in copies:
        copy.wait()


def forward(cols, outw, down, hidden, ids, boxes, cotangent, vec):
    anywhere = pl.BlockSpec(memory_space=pl.ANY)
    vmem = pl.BlockSpec(memory_space=pltpu.VMEM)
    dma = pltpu.SemaphoreType.DMA
    low, wide = jnp.bfloat16, jnp.float32
    page = (TOKENS, WIDE)
    outs = [
        ((12, WIDE, WIDE), low),
        (page, wide),
        ((WIDE, TOKENS), low),
        (page, low),
        (page, low),
        ((WIDE, TOKENS), low),
        (page, low),
        (page, low),
        ((H, 1, TOKENS), wide),
        ((WIDE, TOKENS), low),
        (page, wide),
        ((TOKENS, 128), wide),
        ((4,) + page, low),
        ((4,) + page, wide),
        (page, wide),
        ((16, WIDE), wide),
    ]
    return pl.pallas_call(
        forward_kernel,
        name="forward",
        out_shape=[jax.ShapeDtypeStruct(*o) for o in outs],
        in_specs=[anywhere] * 3 + [vmem] * 5,
        out_specs=[anywhere] * len(outs),
        scratch_shapes=[
            pltpu.VMEM((12, WIDE, WIDE), low),
            pltpu.VMEM((WIDE, TOKENS), low),
            pltpu.VMEM((WIDE, TOKENS), low),
            pltpu.VMEM((WIDE, TOKENS), low),
            pltpu.VMEM(page, wide),
            pltpu.VMEM(page, low),
            pltpu.VMEM(page, low),
            pltpu.VMEM(page, low),
            pltpu.VMEM(page, low),
            pltpu.VMEM((WIDE, TOKENS), low),
            pltpu.VMEM((WIDE, TOKENS), low),
            pltpu.VMEM(page, low),
            pltpu.VMEM((H, 1, TOKENS), wide),
            pltpu.VMEM(page, wide),
            pltpu.VMEM(page, wide),
            pltpu.VMEM(page, low),
            pltpu.VMEM(page, wide),
            pltpu.VMEM((TOKENS, 128), wide),
            pltpu.VMEM((4,) + page, low),
            pltpu.VMEM((2, TOKENS, 256), wide),
            pltpu.VMEM(page, wide),
            pltpu.VMEM(page, wide),
            pltpu.VMEM((16, WIDE), wide),
            dma((12,)),
            dma((12,)),
            dma((4, 4, 12)),
            dma((4, 12)),
            dma((4, 12)),
            dma((14,)),
            dma((20,)),
        ],
        compiler_params=pltpu.CompilerParams(
            collective_id=1, has_side_effects=True, vmem_limit_bytes=61 << 20
        ),
    )(cols, outw, down, hidden, ids, boxes, cotangent, vec)


KEPT = ((8, 5, 9, 4, 0, 1), (3, 10, 11, 6, 7, 2))
EARLY = (((0, 8), (0, 3)), ((1, 5), (1, 10)), ((2, 9), (2, 11)), ((3, 4), (3, 6)), (None, (4, 7)))
LATE = (((4, 0), (5, 2)), ((5, 1), None))
UNIT_ORDER = (0, 2, 1, 3)
RING = 3


def pick(values, e):
    out = values[0]
    for at in range(1, len(values)):
        if values[at] != values[at - 1]:
            out = out + (values[at] - values[at - 1]) * lax.div(e + 8 - at, 8)
    return out


def attend_pair_back(t, q8, k, v, ctx_grad, k_t, stat, dq_t, dk, dv):
    at = columns(t, 128)
    keys, queries, values, grads = k[:, at], q8[:, at], v[:, at], ctx_grad[:, at]
    none = jnp.zeros_like(queries)
    key_sum = value_sum = None
    for e in range(2):
        mask = half_mask(e, queries.shape)
        own_q = jnp.where(mask, queries, none)
        own_g = jnp.where(mask, grads, none)
        probs = jnp.exp(dot_nt(keys, own_q) - stat[2 * t + e])
        prob_grad = dot_nt(values, own_g)
        carried = jnp.sum(probs * prob_grad, 0, keepdims=True)
        score_grad = (probs * (prob_grad - carried)).astype(jnp.bfloat16)
        rows = pl.ds(pl.multiple_of(t * 128 + e * 64, 64), 64)
        dq_t[rows, :] = (dot(k_t[rows, :], score_grad) * HD ** (-0.5)).astype(jnp.bfloat16)
        key_part = dot(score_grad, own_q)
        value_part = dot(probs.astype(jnp.bfloat16), own_g)
        key_sum = key_part if e == 0 else key_sum + key_part
        value_sum = value_part if e == 0 else value_sum + value_part
    dk[:, at] = key_sum.astype(jnp.bfloat16)
    dv[:, at] = value_sum.astype(jnp.bfloat16)


class Stream:
    def __init__(self, entries, chunk, lag, refs, ring, place):
        self.z, self.core, self.x, self.y, self.d = place
        self.p = 2 * self.y + self.x
        self.chunk, self.per, self.lag = chunk, WIDE // chunk, lag
        self.count = len(entries) * self.per
        self.entries, self.refs, self.ring = entries, refs, ring
        self.steps = self.count + 6 * lag + 5

    def where(self, m):
        e, r = lax.div(m, self.per), lax.rem(m, self.per)
        slots = [[(0, 0, -1) if item is None else (item[0], item[1], 1) for item in (pair[c] for pair in self.entries)] for c in range(2)]

        def both(function):
            a = pick([function(item) for item in slots[0]], e)
            b = pick([function(item) for item in slots[1]], e)
            return a + self.core * (b - a)

        q = both(lambda item: item[0])
        j = both(lambda item: item[1] // 4)
        i = both(lambda item: item[1] % 2)
        live = both(lambda item: item[2])
        return q, j, i, r, live

    def rows(self, r):
        return pl.ds(pl.multiple_of(r * self.chunk, self.chunk), self.chunk)

    def remote(self, source, dest, send_sem, recv_sem, device):
        return pltpu.make_async_remote_copy(
            src_ref=source, dst_ref=dest, send_sem=send_sem, recv_sem=recv_sem,
            device_id=device, device_id_type=MESH,
        )

    def role(self, j, r):
        jx, jy = lax.rem(j, 2), lax.div(j, 2)
        rx = self.x + jx - 2 * self.x * jx
        ry = self.y + jy - 2 * self.y * jy
        odd = lax.rem(r, 2)
        first = rx + odd - 2 * rx * odd
        second = ry + odd - 2 * ry * odd
        even_code = 3 - 3 * rx - ry + 2 * rx * ry
        odd_code = 3 - 3 * ry - rx + 2 * rx * ry
        return even_code + odd * (odd_code - even_code), odd

    def along(self, pos, odd):
        turn = odd if pos != 1 else 1 - odd
        return (self.d + turn * (2 - 4 * self.x) + (1 - turn) * (4 - 8 * self.y), self.z)

    def forward(self, q, r, pos, odd):
        R = self.refs
        at = self.rows(r)
        return self.remote(R["mine"].at[q, at, :], R["land"].at[q, at, :], R["send"].at[q, r], R["recv"].at[q, r], self.along(pos, odd))

    def landed(self, q, r):
        R = self.refs
        at = self.rows(r)
        return self.remote(R["land"].at[q, at, :], R["land"].at[q, at, :], R["send"].at[q, r], R["recv"].at[q, r], (self.d, self.z))

    def chained(self, i, r, way):
        R = self.refs
        at = self.rows(r)
        ref = R["chain"].at[way, i, at, :]
        return ref, R["chain_send"].at[way, i, r], R["chain_recv"].at[way, i, r]

    def pass_on(self, source, i, r, way):
        ref, ssem, rsem = self.chained(i, r, way)
        return self.remote(source, ref, ssem, rsem, (self.d, self.z + (1 if way == 0 else -1)))

    def total_out(self, source, i, r):
        R = self.refs
        return pltpu.make_async_copy(source, R["total"].at[i, self.rows(r), :], R["out"].at[i, r])

    def add_to_mine(self, q, r, ref):
        at = self.rows(r)
        mine = self.refs["mine"]
        mine[q, at, :] = (mine[q, at, :].astype(jnp.float32) + ref[...].astype(jnp.float32)).astype(jnp.bfloat16)

    def guarded(self, m, function):
        @pl.when((m >= 0) & (m < self.count))
        def _():
            q, j, i, r, live = self.where(m)

            @pl.when(live > 0)
            def _():
                function(m, q, j, i, r)


    def begin_pair(self, m, q, j, i, r):
        R = self.refs
        quarter = 256 // self.chunk

        @pl.when(lax.rem(r, quarter) == 0)
        def _():
            f = lax.div(r, quarter)
            at = pl.ds(pl.multiple_of(f * 256, 256), 256)
            self.remote(R["sib"].at[q, at, :], R["sib"].at[q, at, :], R["give_send"].at[q, f], R["give_recv"].at[q, f], (self.d, self.z)).wait_recv()

        slot = lax.rem(m, 2)
        pltpu.make_async_copy(R["sib"].at[q, self.rows(r), :], self.ring.at[0, slot], R["ring_sem"].at[0, slot]).start()

    def end_pair(self, m, q, j, i, r):
        R = self.refs
        slot = lax.rem(m, 2)
        pltpu.make_async_copy(R["sib"].at[q, self.rows(r), :], self.ring.at[0, slot], R["ring_sem"].at[0, slot]).wait()
        self.add_to_mine(q, r, self.ring.at[0, slot])
        pos, odd = self.role(j, r)

        @pl.when(pos == 0)
        def _():
            self.forward(q, r, 0, odd).start()

    def begin_path(self, step_pos):
        def run(m, q, j, i, r):
            pos, odd = self.role(j, r)
            R = self.refs

            @pl.when(pos == step_pos)
            def _():
                slot = lax.rem(m, 2)
                self.landed(q, r).wait_recv()
                pltpu.make_async_copy(R["land"].at[q, self.rows(r), :], self.ring.at[step_pos, slot], R["ring_sem"].at[step_pos, slot]).start()

        return run

    def end_path(self, step_pos):
        def run(m, q, j, i, r):
            pos, odd = self.role(j, r)
            R = self.refs

            @pl.when(pos == step_pos)
            def _():
                slot = lax.rem(m, 2)
                pltpu.make_async_copy(R["land"].at[q, self.rows(r), :], self.ring.at[step_pos, slot], R["ring_sem"].at[step_pos, slot]).wait()
                self.add_to_mine(q, r, self.ring.at[step_pos, slot])
                if step_pos < 3:
                    self.forward(q, r, step_pos, odd).start()
                else:
                    mine = R["mine"].at[q, self.rows(r), :]

                    @pl.when(self.z == 0)
                    def _():
                        self.pass_on(mine, i, r, 0).start()

                    @pl.when(self.z == 3)
                    def _():
                        self.pass_on(mine, i, r, 1).start()

        return run

    def link(self, q, i, r, way, last):
        R = self.refs
        at = self.rows(r)
        ref, ssem, rsem = self.chained(i, r, way)
        self.remote(ref, ref, ssem, rsem, (self.d, self.z)).wait_recv()
        came = ref[...].astype(jnp.float32)
        mine = R["mine"]
        ref[...] = (mine[q, at, :].astype(jnp.float32) + came).astype(jnp.bfloat16)
        self.pass_on(ref, i, r, way).start()
        if last:
            other = R["chain"][1 - way, i, at, :].astype(jnp.float32)
            mine[q, at, :] = (other + came).astype(jnp.bfloat16)
            self.total_out(mine.at[q, at, :], i, r).start()

    def links(self, last):
        def run(m, q, j, i, r):
            for z, way in ((1, 1 if last else 0), (2, 0 if last else 1)):

                @pl.when((self.p == j) & (self.z == z))
                def _(way=way):
                    self.link(q, i, r, way, last)

        return run

    def ends(self, m, q, j, i, r):
        R = self.refs
        at = self.rows(r)
        for z, way in ((0, 1), (3, 0)):

            @pl.when((self.p == j) & (self.z == z))
            def _(way=way):
                ref, ssem, rsem = self.chained(i, r, way)
                self.remote(ref, ref, ssem, rsem, (self.d, self.z)).wait_recv()
                ref[...] = (R["mine"][q, at, :].astype(jnp.float32) + ref[...].astype(jnp.float32)).astype(jnp.bfloat16)
                self.total_out(ref, i, r).start()

    def step(self, n):
        L = self.lag
        parts = [
            (0, self.begin_pair),
            (1, self.end_pair),
            (1 + L, self.begin_path(1)),
            (2 + L, self.end_path(1)),
            (2 + 2 * L, self.begin_path(2)),
            (3 + 2 * L, self.end_path(2)),
            (3 + 3 * L, self.begin_path(3)),
            (4 + 3 * L, self.end_path(3)),
            (4 + 4 * L, self.links(False)),
            (4 + 5 * L, self.links(True)),
            (4 + 6 * L, self.ends),
        ]
        for lag, part in reversed(parts):
            self.guarded(n - lag, part)

    def finish(self, m):
        def run(m, q, j, i, r):
            pos, odd = self.role(j, r)

            @pl.when(pos < 3)
            def _():
                self.forward(q, r, 0, odd).wait_send()

            mine = self.refs["mine"].at[q, self.rows(r), :]

            @pl.when((pos == 3) & (self.z < 3))
            def _():
                self.pass_on(mine, i, r, 0).wait_send()

            @pl.when((pos == 3) & (self.z > 0))
            def _():
                self.pass_on(mine, i, r, 1).wait_send()

            @pl.when(pos == 3)
            def _():
                self.total_out(mine, i, r).wait()

        self.guarded(m, run)


def backward_kernel(
    full, x_in, q_in, k_in, kt_in, v_in, ctx_in, stat_in, mid_in, hat_in, inv_in, act_in, slope_in, two_in, sums_in, vec,
    input_out, total, sums, sib, land,
    w, pb, pt, pf, stat, inv, stage, mine, chain, ring_a, ring_b, vec_in,
    wsem, asem, ssem, isem, osem,
    give_send, give_recv, send_a, recv_a, chain_send_a, chain_recv_a, out_a, ring_sem_a,
    send_b, recv_b, chain_send_b, chain_recv_b, out_b, ring_sem_b, vec_send, vec_recv,
):
    z, core, x, y, near = position()
    p = 2 * y + x
    d = 2 * p + core
    z_one = (d, z + 1 - 2 * (z % 2))
    z_two = (d, z + 2 - 4 * (z // 2))
    shared = {"mine": mine, "land": land, "chain": chain, "sib": sib, "total": total, "give_send": give_send, "give_recv": give_recv}
    place = (z, core, x, y, d)
    early = Stream(EARLY, CHUNK_EARLY, LAG_EARLY, dict(
        shared, send=send_a, recv=recv_a, chain_send=chain_send_a, chain_recv=chain_recv_a, out=out_a, ring_sem=ring_sem_a,
    ), ring_a, place)
    late = Stream(LATE, CHUNK_LATE, LAG_LATE, dict(
        shared, send=send_b, recv=recv_b, chain_send=chain_send_b, chain_recv=chain_recv_b, out=out_b, ring_sem=ring_sem_b,
    ), ring_b, place)

    two_low, act_ring, up_grad = pb.at[0], (pb.at[1], pb.at[2]), pb.at[3]
    k, q8, v = pb.at[4], pb.at[5], pb.at[6]
    one_low, ctx, ctx_grad, dq, dk, dv = pb.at[0], pb.at[1], pb.at[2], pb.at[0], pb.at[1], pb.at[3]
    two_t, mid_t, k_t = pt.at[0], pt.at[1], pt.at[2]
    one_t, x_t, dq_t = pt.at[0], pt.at[1], pt.at[0]
    two, back, slope_ring = pf.at[0], pf.at[1], (pf.at[2], pf.at[3])
    one, hat = pf.at[0], pf.at[2]
    uses = [slot for u in UNIT_ORDER for slot in (8 + u, 3 + u)] + [7, 0, 1, 2]

    def weight(n):
        return pltpu.make_async_copy(full.at[uses[n]], w.at[n % RING], wsem.at[n % RING])

    def act_load(n):
        return pltpu.make_async_copy(act_in.at[UNIT_ORDER[n]], act_ring[n % 2], asem.at[n % 2])

    def slope_load(n):
        return pltpu.make_async_copy(slope_in.at[UNIT_ORDER[n]], slope_ring[n % 2], ssem.at[n % 2])

    loads = {}

    def fetch(name, source, dest):
        loads[name] = pltpu.make_async_copy(source, dest, isem.at[len(loads)])
        loads[name].start()

    fetch("two", two_in, two)
    weight(0).start()
    slope_load(0).start()
    act_load(0).start()
    fetch("mid", mid_in, mid_t)
    weight(1).start()
    fetch("sums", sums_in, sums)
    weight(2).start()
    slope_load(1).start()
    act_load(1).start()
    for name, source, dest in (
        ("inv", inv_in, inv), ("k", k_in, k), ("q", q_in, q8), ("v", v_in, v), ("kt", kt_in, k_t), ("stat", stat_in, stat),
    ):
        fetch(name, source, dest)
    meet(z, near, (z_two,))

    counter = {"early": 0, "late": 0, "whole": 0}
    produced = set()

    def run(count, body, per=0, every=1, stream=early, name="early"):
        base = counter[name]
        total_steps = (count // every) * per

        def one_turn(i):
            body(i)
            if per:
                if every == 1:
                    for s in range(per):
                        stream.step(base + i * per + s)
                else:

                    @pl.when(lax.rem(i, every) == every - 1)
                    def _():
                        for s in range(per):
                            stream.step(base + lax.div(i, every) * per + s)

        if per:
            have = 0
            for pair in stream.entries:
                if all(item is None or item[1] in produced for item in pair):
                    have += 1
                else:
                    break
            limit = stream.steps if have == len(stream.entries) else have * stream.per
            assert base + total_steps <= limit, (name, base, total_steps, limit)
        loop(count, one_turn)
        counter[name] = base + total_steps

    def use(n):
        weight(n).wait()
        return w.at[n % RING]

    def done(n):
        if n + RING < 12:
            weight(n + RING).start()

    given = {0: [], 1: []}

    def give(slot, c, n, f):
        at = pl.ds(f * 256, 256)
        q = KEPT[1 - c].index(slot)
        return pltpu.make_async_remote_copy(
            src_ref=stage.at[n % 2, at, :], dst_ref=sib.at[q, at, :], send_sem=give_send.at[q, f],
            recv_sem=give_recv.at[q, f], device_id=near["c"], device_id_type=MESH,
        )

    def block(slot, left_t, right, **steps):
        owner = (slot // 2) % 2
        giver = 1 - owner
        q = KEPT[owner].index(slot)
        n = len(given[giver])
        if n >= 2:

            @pl.when(core == giver)
            def _():
                for f in range(4):
                    give(given[giver][n - 2], giver, n - 2, f).wait_send()

        def tile(i):
            value = dot(left_t[...], right[:, columns(i)]).astype(jnp.bfloat16)

            @pl.when(core == owner)
            def _():
                mine[q, :, columns(i)] = value

            @pl.when(core == giver)
            def _():
                stage[n % 2, :, columns(i)] = value

        run(WIDE // 256, tile, **steps)

        @pl.when(core == giver)
        def _():
            for f in range(4):
                give(slot, giver, n, f).start()

        given[giver].append(slot)
        produced.add(slot)

    def token_sum(row, ref):
        def tile(i):
            at = columns(i)
            sums[row : row + 1, at] = jnp.sum(ref[:, at].astype(jnp.float32), 0, keepdims=True)

        loop(WIDE // 256, tile)

    @pl.when(p == 3)
    def _():
        chain[0] = jnp.zeros(chain.shape[1:], chain.dtype)
        pltpu.make_async_copy(chain.at[0], total, osem.at[1]).start()

    loads["two"].wait()

    def to_low(r):
        two_low[r, :] = two[r, :].astype(jnp.bfloat16)

    row_loop(to_low)
    transpose_into(two_t, two_low)
    loads["mid"].wait()
    loads["sums"].wait()
    for n, u in enumerate(UNIT_ORDER):
        pace = PACE[n]
        weights = use(2 * n)
        slope_load(n).wait()
        act_load(n).wait()
        slope = slope_ring[n % 2]

        def tile(i):
            rows = columns(i)
            grad = dot_nt(two_low[...], weights[rows, :]) * slope[:, rows]
            up_grad[:, rows] = grad.astype(jnp.bfloat16)

        run(WIDE // 256, tile, **pace[0])
        done(2 * n)
        if n == 2:
            fetch("hat", hat_in, hat)
        token_sum(8 + u, up_grad)
        block(8 + u, two_t, act_ring[n % 2], **pace[1])
        if n == 2:
            fetch("ctx", ctx_in, ctx)
        weights = use(2 * n + 1)

        def tile_back(i):
            at = columns(i)
            value = dot_nt(up_grad[...], weights[at, :])
            back[:, at] = two[:, at] + value if n == 0 else back[:, at] + value

        run(WIDE // 256, tile_back, **pace[2])
        done(2 * n + 1)
        block(3 + u, mid_t, up_grad, **pace[3])
        if n + 2 < 4:
            slope_load(n + 2).start()
            act_load(n + 2).start()
    fetch("x", x_in, x_t)
    for name in ("hat", "inv"):
        loads[name].wait()
    sums[0:1, :] = jnp.zeros((1, WIDE), jnp.float32)
    sums[2:4, :] = jnp.zeros((2, WIDE), jnp.float32)

    def rows(i):
        r = pl.ds(pl.multiple_of(i * SLICE, SLICE), SLICE)
        grad, normed = back[r, :], hat[r, :]
        scaled = grad * vec[2:3, :]
        arg = inv[r, 0:1] * (scaled - mean_of(scaled) - normed * mean_of(scaled * normed))
        one[r, :] = arg
        one_low[r, :] = arg.astype(jnp.bfloat16)
        sums[0:1, :] += jnp.sum(arg, 0, keepdims=True)
        sums[2:3, :] += jnp.sum(grad * normed, 0, keepdims=True)
        sums[3:4, :] += jnp.sum(grad, 0, keepdims=True)

    run(TOKENS // SLICE, rows, **PACE[4])
    transpose_into(one_t, one_low)
    weights = use(8)

    def tile_ctx(i):
        at = columns(i)
        ctx_grad[:, at] = dot_nt(one_low[...], weights[at, :]).astype(jnp.bfloat16)

    run(WIDE // 256, tile_ctx, **PACE[5])
    done(8)
    loads["ctx"].wait()
    block(7, one_t, ctx, **PACE[6])
    for name in ("k", "q", "v", "kt", "stat"):
        loads[name].wait()
    run(H // 2, lambda t: attend_pair_back(t, q8, k, v, ctx_grad, k_t, stat, dq_t, dk, dv), **PACE[7])
    transpose_back(dq, dq_t)
    loads["x"].wait()
    block(0, x_t, dq, **PACE[8])
    block(2, x_t, dv, **PACE[8])
    block(1, x_t, dk, **PACE[8])

    def vec_hop(h):
        device = (near["c"], near["x"], near["y"], z_one, z_two)[h]
        return pltpu.make_async_remote_copy(
            src_ref=sums, dst_ref=vec_in.at[h], send_sem=vec_send.at[h], recv_sem=vec_recv.at[h],
            device_id=device, device_id_type=MESH,
        )

    token_sum(6, dq)
    token_sum(7, dv)
    vec_hop(0).start()
    hop = 0
    tail = {"early": counter["early"], "late": 0}

    def both(count, rate, body=None):
        base_late, base_early = tail["late"], tail["early"]

        def turn(i):
            if body is not None:
                body(i)

            for s in range(rate):
                early.step(base_early + i * rate + s)
            late.step(base_late + i)

        loop(count, turn)
        tail["late"] += count
        tail["early"] += count * rate

    for kk, grad in ((0, dq), (1, dk), (2, dv)):
        weights = use(9 + kk)

        def tile_in(i):
            at = columns(i)
            one[:, at] = one[:, at] + dot_nt(grad[...], weights[at, :])

        both(WIDE // 256, EARLY_RATE, tile_in)
    out = pltpu.make_async_copy(one, input_out, osem.at[0])
    out.start()
    for h in range(5):
        vec_hop(h).wait()
        sums[...] = sums[...] + vec_in[h]
        if h < 4:
            vec_hop(h + 1).start()
            both(4, EARLY_RATE)
    left = max(0, -(-(early.steps - tail["early"]) // EARLY_RATE))
    both(min(left, late.steps - tail["late"]), EARLY_RATE)
    loop(late.steps - tail["late"], lambda i, base=tail["late"]: late.step(base + i))
    assert tail["early"] >= early.steps

    for c in range(2):

        @pl.when(core == c)
        def _(c=c):
            n = len(given[c])
            for back_by in (2, 1):
                for f in range(4):
                    give(given[c][n - back_by], c, n - back_by, f).wait_send()

    loop(early.count, early.finish)
    loop(late.count, late.finish)
    out.wait()

    @pl.when(p == 3)
    def _():
        pltpu.make_async_copy(chain.at[0], total, osem.at[1]).wait()


CHUNK_EARLY, CHUNK_LATE = 128, 64
LAG_EARLY, LAG_LATE = 2, 3
EARLY_RATE = 1
NO = {}
SLOW = {"per": 1, "every": 2}
ONE = {"per": 1}
PACE = (
    (NO, NO, NO, NO),
    (SLOW, SLOW, SLOW, SLOW),
    (SLOW, SLOW, SLOW, SLOW),
    (NO, NO, SLOW, SLOW),
    {"per": 1, "every": 4},
    SLOW,
    SLOW,
    {"per": 1, "every": 2},
    SLOW,
)


def backward(full, x, q, k, kt, v, ctx, stat, mid, hat, inv, act, slope, two, sums, vec):
    anywhere = pl.BlockSpec(memory_space=pl.ANY)
    vmem = pl.BlockSpec(memory_space=pltpu.VMEM)
    dma = pltpu.SemaphoreType.DMA
    low, wide = jnp.bfloat16, jnp.float32
    page = (TOKENS, WIDE)
    many_a, many_b = WIDE // CHUNK_EARLY, WIDE // CHUNK_LATE

    def stream_sems(many):
        return [dma((6, many)), dma((6, many)), dma((2, 2, many)), dma((2, 2, many)), dma((2, many)), dma((4, 2))]

    return pl.pallas_call(
        backward_kernel,
        name="backward",
        out_shape=[
            jax.ShapeDtypeStruct(page, wide),
            jax.ShapeDtypeStruct((2, WIDE, WIDE), low),
            jax.ShapeDtypeStruct((16, WIDE), wide),
            jax.ShapeDtypeStruct((6, WIDE, WIDE), low),
            jax.ShapeDtypeStruct((6, WIDE, WIDE), low),
        ],
        in_specs=[anywhere] * 15 + [vmem],
        out_specs=[anywhere, anywhere, vmem, anywhere, anywhere],
        scratch_shapes=[
            pltpu.VMEM((RING, WIDE, WIDE), low),
            pltpu.VMEM((7,) + page, low),
            pltpu.VMEM((3, WIDE, TOKENS), low),
            pltpu.VMEM((4,) + page, wide),
            pltpu.VMEM((H, 1, TOKENS), wide),
            pltpu.VMEM((TOKENS, 128), wide),
            pltpu.VMEM((2, WIDE, WIDE), low),
            pltpu.VMEM((6, WIDE, WIDE), low),
            pltpu.VMEM((2, 2, WIDE, WIDE), low),
            pltpu.VMEM((4, 2, CHUNK_EARLY, WIDE), low),
            pltpu.VMEM((4, 2, CHUNK_LATE, WIDE), low),
            pltpu.VMEM((5, 16, WIDE), wide),
            dma((RING,)), dma((2,)), dma((2,)), dma((12,)), dma((2,)),
            dma((6, 4)), dma((6, 4)),
            *stream_sems(many_a),
            *stream_sems(many_b),
            dma((5,)), dma((5,)),
        ],
        compiler_params=pltpu.CompilerParams(
            collective_id=2, has_side_effects=True, vmem_limit_bytes=62 << 20
        ),
    )(full, x, q, k, kt, v, ctx, stat, mid, hat, inv, act, slope, two, sums, vec)


def layout_embed(cell_boxes, cell_ids):
    cell_count = cell_boxes.shape[1]
    onehot = (
        cell_ids[:, :, None] == jnp.arange(cell_count, dtype=jnp.int32)[None, None, :]
    ).astype(jnp.float32)
    corners = jnp.einsum("psc,pck->psk", onehot, cell_boxes.astype(jnp.float32), precision=PRECISE)
    quarter = MODEL_WIDTH // 4
    half_width = quarter // 2
    frequency = jnp.exp(
        -jnp.arange(half_width, dtype=jnp.float32) * (math.log(1000.0) / half_width)
    )
    angle_grid = corners[..., None] * frequency
    wave_table = jnp.concatenate([jnp.sin(angle_grid), jnp.cos(angle_grid)], -1)
    return 0.5 * wave_table.reshape(corners.shape[0], corners.shape[1], MODEL_WIDTH)


def gelu_exact(values):
    return jax.nn.gelu(values, approximate=False)


def norm_forward(values, gain, shift):
    center = values - jnp.mean(values, -1, keepdims=True)
    inv_std = lax.rsqrt(jnp.mean(center * center, -1, keepdims=True) + EPS_NORM)
    normed = center * inv_std
    return (normed * gain + shift, normed, inv_std)


def norm_backward(grad_in, normed, inv_std, gain):
    scaled = grad_in * gain
    grad_arg = inv_std * (
        scaled
        - jnp.mean(scaled, -1, keepdims=True)
        - normed * jnp.mean(scaled * normed, -1, keepdims=True)
    )
    return (grad_arg, jnp.sum(grad_in * normed, (0, 1)), jnp.sum(grad_in, (0, 1)))


def attend(query_low, key_low, value_low, head_count):
    groups, seq_len = (query_low.shape[0], query_low.shape[1])
    shape_heads = (groups, seq_len, head_count, HD)
    scores = jnp.einsum(
        "gqhe,gkhe->ghqk",
        query_low.reshape(shape_heads),
        key_low.reshape(shape_heads),
        preferred_element_type=jnp.float32,
    ) * HD ** (-0.5)
    row_max = jnp.max(scores, -1, keepdims=True)
    log_total = row_max + jnp.log(jnp.sum(jnp.exp(scores - row_max), -1, keepdims=True))
    probs = jnp.exp(scores - log_total).astype(jnp.bfloat16)
    context = jnp.einsum(
        "ghqk,gkhe->gqhe", probs, value_low.reshape(shape_heads), preferred_element_type=jnp.float32
    )
    return (context.reshape(groups, seq_len, head_count * HD).astype(jnp.bfloat16), log_total)


def attend_back(query_low, key_low, value_low, log_total, ctx_grad, head_count):
    groups, seq_len = (query_low.shape[0], query_low.shape[1])
    shape_heads = (groups, seq_len, head_count, HD)
    query_heads = query_low.reshape(shape_heads)
    key_heads = key_low.reshape(shape_heads)
    value_heads = value_low.reshape(shape_heads)
    grad_heads = ctx_grad.reshape(shape_heads)
    scale = HD ** (-0.5)
    scores = (
        jnp.einsum("gqhe,gkhe->ghqk", query_heads, key_heads, preferred_element_type=jnp.float32)
        * scale
    )
    probs = jnp.exp(scores - log_total)
    value_grad = jnp.einsum(
        "ghqk,gqhe->gkhe",
        probs.astype(jnp.bfloat16),
        grad_heads,
        preferred_element_type=jnp.float32,
    )
    prob_grad = jnp.einsum(
        "gqhe,gkhe->ghqk", grad_heads, value_heads, preferred_element_type=jnp.float32
    )
    score_grad = (probs * (prob_grad - jnp.sum(probs * prob_grad, -1, keepdims=True))).astype(
        jnp.bfloat16
    )
    query_grad = (
        jnp.einsum("ghqk,gkhe->gqhe", score_grad, key_heads, preferred_element_type=jnp.float32)
        * scale
    )
    key_grad = (
        jnp.einsum("ghqk,gqhe->gkhe", score_grad, query_heads, preferred_element_type=jnp.float32)
        * scale
    )
    width = head_count * HD
    return (
        query_grad.reshape(groups, seq_len, width).astype(jnp.bfloat16),
        key_grad.reshape(groups, seq_len, width).astype(jnp.bfloat16),
        value_grad.reshape(groups, seq_len, width).astype(jnp.bfloat16),
    )


def by_collectives(
    hidden, cell_ids, cell_boxes, cotangent, weight_cols, weight_out, weight_down, vectors, slot_dev
):
    dp_count = lax.axis_size("dp")
    col_mats = lax.all_gather(weight_cols, "tp", axis=2, tiled=True)
    out_mat = lax.all_gather(weight_out, "tp", axis=0, tiled=True)
    down_mats = lax.all_gather(weight_down, "tp", axis=1, tiled=True)
    x_own = hidden.astype(jnp.float32) + layout_embed(cell_boxes, cell_ids)
    x_low = x_own.astype(jnp.bfloat16)
    projected = jnp.einsum(
        "gtd,kdc->kgtc", x_low, col_mats[0:3], preferred_element_type=jnp.float32
    )
    query_low = (projected[0] + vectors[:, 6]).astype(jnp.bfloat16)
    key_low = projected[1].astype(jnp.bfloat16)
    value_low = (projected[2] + vectors[:, 7]).astype(jnp.bfloat16)
    context, log_total = attend(query_low, key_low, value_low, H)
    attn_out = jnp.einsum("gtc,cd->gtd", context, out_mat, preferred_element_type=jnp.float32)
    mid_out, mid_hat, mid_inv = norm_forward(
        x_own + attn_out + vectors[:, 0], vectors[:, 2], vectors[:, 3]
    )
    mid_low = mid_out.astype(jnp.bfloat16)
    up_pre = jnp.einsum(
        "gtd,kdc->kgtc", mid_low, col_mats[3:7], preferred_element_type=jnp.float32
    )
    up_pre = up_pre + jnp.transpose(vectors[:, 8:12])[:, None, None, :]
    act_low = gelu_exact(up_pre).astype(jnp.bfloat16)
    ffn_out = jnp.einsum("kgtc,kcd->gtd", act_low, down_mats, preferred_element_type=jnp.float32)
    layer_out, out_hat, out_inv = norm_forward(
        mid_out + ffn_out + vectors[:, 1], vectors[:, 4], vectors[:, 5]
    )
    output_gradient = cotangent.astype(jnp.float32)
    grad_two, gain_two, shift_two = norm_backward(output_gradient, out_hat, out_inv, vectors[:, 4])
    two_low = grad_two.astype(jnp.bfloat16)
    act_grad = jnp.einsum("gtd,kcd->kgtc", two_low, down_mats, preferred_element_type=jnp.float32)
    gelu_pull = jax.vjp(gelu_exact, up_pre)[1]
    up_low = gelu_pull(act_grad)[0].astype(jnp.bfloat16)
    mid_back = jnp.einsum(
        "kgtc,kdc->gtd", up_low, col_mats[3:7], preferred_element_type=jnp.float32
    )
    grad_one, gain_one, shift_one = norm_backward(
        mid_back + grad_two, mid_hat, mid_inv, vectors[:, 2]
    )
    one_low = grad_one.astype(jnp.bfloat16)
    ctx_grad = jnp.einsum(
        "gtd,cd->gtc", one_low, out_mat, preferred_element_type=jnp.float32
    ).astype(jnp.bfloat16)
    query_grad, key_grad, value_grad = attend_back(
        query_low, key_low, value_low, log_total, ctx_grad, H
    )
    qkv_grad = jnp.stack([query_grad, key_grad, value_grad], 0)
    input_grad = grad_one + jnp.einsum(
        "kgtc,kdc->gtd", qkv_grad, col_mats[0:3], preferred_element_type=jnp.float32
    )

    def block(text, left, right):
        return jnp.einsum(text, left, right, preferred_element_type=jnp.float32).astype(
            jnp.bfloat16
        )

    qkv_blocks = block("gtd,kgtc->kdc", x_low, qkv_grad)
    up_blocks = block("gtd,kgtc->kdc", mid_low, up_low)
    out_block = block("gtd,gtc->dc", one_low, context)[None]
    down_blocks = block("gtd,kgtc->kdc", two_low, act_low)
    vector_part = jnp.stack(
        [
            jnp.sum(grad_one, (0, 1)),
            jnp.sum(grad_two, (0, 1)),
            gain_one,
            shift_one,
            gain_two,
            shift_two,
            jnp.sum(query_grad, (0, 1), dtype=jnp.float32),
            jnp.sum(value_grad, (0, 1), dtype=jnp.float32),
        ],
        0,
    )
    vector_part = jnp.concatenate(
        [vector_part, jnp.sum(up_low, (1, 2), dtype=jnp.float32)], 0
    )
    block_part = jnp.concatenate(
        [
            qkv_blocks,
            up_blocks,
            out_block,
            down_blocks,
            jnp.zeros((slot_dev * dp_count - 12, MODEL_WIDTH, MODEL_WIDTH), jnp.bfloat16),
        ],
        0,
    )
    block_owned = lax.psum_scatter(block_part, "dp", scatter_dimension=0, tiled=True)
    full_grad = lax.psum(block_owned, "tp")
    vector_all = lax.psum(vector_part, ("dp", "tp"))
    return layer_out, input_grad, full_grad, vector_all


def local(
    hidden,
    cell_ids,
    cell_boxes,
    cotangent,
    weight_cols,
    weight_out,
    weight_down,
    vectors,
    vector_moment,
    left_stat,
    right_stat,
    left_root,
    right_root,
    master,
    averaged_weight,
):
    tp_count = lax.axis_size("tp")
    dp_count = lax.axis_size("dp")
    tp_index = lax.axis_index("tp")
    dp_index = lax.axis_index("dp")
    strip_width = weight_cols.shape[2]
    page_rows, seq_len = (hidden.shape[0], hidden.shape[1])
    owned_rows = vector_moment.shape[0]
    slot_dev = left_stat.shape[0]
    if dp_count == 8 and tp_count == 4:
        vec = jnp.transpose(vectors)
        full, layer_out, *kept, sums = forward(
            weight_cols, weight_out, weight_down, hidden[0], cell_ids, cell_boxes[0], cotangent[0], vec
        )
        input_grad, full_grad, vector_all, *_ = backward(full, *kept, sums, vec)
        layer_out, input_grad = layer_out[None], input_grad[None]
    else:
        layer_out, input_grad, full_grad, vector_all = by_collectives(
            hidden, cell_ids, cell_boxes, cotangent, weight_cols, weight_out, weight_down, vectors, slot_dev
        )
    vector_grad = jnp.transpose(
        lax.dynamic_slice_in_dim(vector_all[0:12], dp_index * owned_rows, owned_rows, 1)
    )
    own_rows = lax.dynamic_slice_in_dim(full_grad, tp_index * strip_width, strip_width, 1)
    own_cols = lax.dynamic_slice_in_dim(full_grad, tp_index * strip_width, strip_width, 2)
    block_grad = own_cols.astype(jnp.float32)
    left_new = STAT_DECAY * left_stat + (1.0 - STAT_DECAY) * jnp.einsum(
        "sic,sjc->sij", own_rows, full_grad, preferred_element_type=jnp.float32
    )
    right_new = STAT_DECAY * right_stat + (1.0 - STAT_DECAY) * jnp.einsum(
        "sic,sij->scj", own_cols, full_grad, preferred_element_type=jnp.float32
    )

    def parts(array):
        high = array.astype(jnp.bfloat16)
        return high, (array - high.astype(jnp.float32)).astype(jnp.bfloat16)

    def product(left, right):
        return jnp.einsum("sij,sjc->sic", left, right, preferred_element_type=jnp.float32)

    left_high, left_rest = parts(left_root)
    right_high, right_rest = parts(right_root)
    precond = product(left_high, full_grad) + product(left_rest, full_grad)
    pre_high, pre_rest = parts(precond)
    precond = (
        product(pre_high, right_high) + product(pre_rest, right_high) + product(pre_high, right_rest)
    )
    master_new = master - BLOCK_RATE * precond
    weight_copy = master_new.astype(jnp.bfloat16)
    ema_new = EMA_DECAY * averaged_weight + (1.0 - EMA_DECAY) * master_new
    vector_rows = lax.dynamic_slice_in_dim(vectors, dp_index * owned_rows, owned_rows, 0)
    moment_new = MOMENTUM * vector_moment + vector_grad
    total_tokens = page_rows * seq_len * dp_count * tp_count
    vector_new = vector_rows - VEC_RATE * lax.rsqrt(jnp.float32(total_tokens)) * moment_new
    bias_grad = vector_grad[:, 0]
    return (
        layer_out,
        input_grad,
        block_grad,
        left_new,
        right_new,
        master_new,
        weight_copy,
        ema_new,
        vector_grad,
        moment_new,
        vector_new,
        bias_grad,
    )


def solution(mesh):
    return jax.shard_map(
        local,
        mesh=mesh,
        in_specs=(
            P(("dp", "tp"), None, None),
            P(("dp", "tp"), None),
            P(("dp", "tp"), None, None),
            P(("dp", "tp"), None, None),
            P(None, None, "tp"),
            P("tp", None),
            P(None, "tp", None),
            P(),
            P("dp", None),
            P("dp", "tp", None),
            P("dp", "tp", None),
            P("dp", "tp", None),
            P("dp", None, None),
            P("dp", "tp", None),
            P("dp", "tp", None),
        ),
        out_specs=(
            P(("dp", "tp"), None, None),
            P(("dp", "tp"), None, None),
            P("dp", None, "tp"),
            P("dp", "tp", None),
            P("dp", "tp", None),
            P("dp", "tp", None),
            P("dp", "tp", None),
            P("dp", "tp", None),
            P("dp", None),
            P("dp", None),
            P("dp", None),
            P("dp"),
        ),
        check_vma=False,
    )
```

profile of v0, /device:TPU:0, one launch (start us, length us, event | category | flops | bytes accessed | tf_op | source)
XLA Modules:
  0.0 435.5 jit_solution(1108759052983385368)
XLA Ops:
  0.6 1.4 copy.27
  2.0 115.1 %forward.1 = (bf16[12,1024,1024]{2,1,0:T(8,128)(2,1)}, f32[512,1024]{1,0:T(8,128)}, bf16[1024,512]{1,0:T(8,128)(2,1)}, bf16[512,1024]{1,0:T(8,128)(2,1)}, bf16[5...) custom-call(bf16[7,1024,256]{2,1,0:T(8,128)(2,1)} %cols.1, ...), custom_call_target="tpu_custom_call" | custom-call | tf_op jit(solution)/shard_map/forward/pallas_call | solution.py:485
  117.1 289.7 %backward.1 = (f32[512,1024]{1,0:T(8,128)}, bf16[2,1024,1024]{2,1,0:T(8,128)(2,1)}, f32[16,1024]{1,0:T(8,128)}, bf16[6,1024,1024]{2,1,0:T(8,128)(2,1)}, bf16[6,1024,1024]{2,1,0:T(8,128)(2,1)}) custom-call(bf16[12,1024,1024]{2,1,0:T(8,128)(2,1)} %get-tuple-element.32.full, bf16[1024,512]{1,0:T(8,128)(2,1)} %get-tuple-element.33.x_in, ...), custom_call_target="tpu_custom_call" | custom-call | tf_op jit(solution)/shard_map/backward/pallas_call | solution.py:1129
  406.8 0.0 copy-start.6
  406.8 2.9 dynamic-slice_convert_fusion
  409.7 5.3 %add_multiply_fusion.1 = f32[2,256,1024]{2,1,0:T(8,128)} fusion(f32[2,256,1024]{2,1,0:T(8,128)S(1)} %copy-done.6, bf16[2,1024,1024]{2,1,0:T(8,128)(2,1)} %get-tuple-element.48, s32[]{:T(128)S(6)} %select_n.8), kind=kOutput, calls=%fused_computation.8 | convolution fusion | flops 1074790400 | bytes 9437188 | tf_op jit(solution)/shard_map/sic,sjc->sij/dot_general | solution.py:1399
  415.0 2.7 add_multiply_fusion
  417.7 1.8 fusion.1
  419.5 0.0 slice-start.1
  419.5 1.8 bitcast_add_fusion
  421.3 0.4 slice-done.1
  421.8 1.3 fusion.11
  423.1 0.0 copy-start.2
  423.1 0.0 copy-start.3
  423.1 1.3 fusion.2
  424.4 0.3 copy-done.2
  424.6 0.6 copy-done.3
  425.3 4.2 multiply_add_fusion
  429.5 0.0 copy-done.8
  429.5 1.3 multiply_subtract_fusion.1
  430.8 0.5 slice_bitcast_fusion
  431.4 1.3 copy.42
  432.7 1.0 copy-done.5
  433.7 1.3 copy.43
  (16 shorter events, 0.0 us)
Async XLA Ops:
  406.8 2.9 copy-start.6
  409.7 5.3 %copy-start = (bf16[2,1024,1024]{2,1,0:T(8,128)(2,1)S(1)}, bf16[2,1024,1024]{2,1,0:T(8,128)(2,1)}, u32[]{:S(2)}) copy-start(bf16[2,1024,1024]{2,1,0:T(8,128)(2,1)} %get-tuple-element.48) | copy-start | bytes 12582916
  409.7 5.3 %copy-start.7 = (f32[2,256,1024]{2,1,0:T(8,128)S(1)}, f32[2,256,1024]{2,1,0:T(8,128)}, u32[]{:S(2)}) copy-start(f32[2,256,1024]{2,1,0:T(8,128)} %param.25) | copy-start | bytes 6291460
  415.0 2.7 copy-start.1
  417.7 3.7 slice-start
  419.5 2.3 slice-start.1
  423.1 1.6 copy-start.2
  423.1 2.2 copy-start.3
  425.3 4.2 copy-start.8
  425.3 6.1 %copy-start.4 = (f32[512,1024]{1,0:T(8,128)S(1)}, f32[512,1024]{1,0:T(8,128)}, u32[]{:S(2)}) copy-start(f32[512,1024]{1,0:T(8,128)} %get-tuple-element.31) | copy-start | bytes 6291460
  430.8 1.8 copy-start.9
  431.3 2.3 copy-start.5
where the time goes:
time: 442 us; the launch traced here: 435 us
  Pallas kernels  405 us (92%)
  matrix products  18.4 us (4%)
  local copies, waits for them, and re-layouts  6.93 us (2%)
    pallas_call x1, Pallas kernels, backward(): pl.pallas_call(backward_kernel, name='backward', out_shape=[jax.ShapeDtyp...  290 us
    pallas_call x1, Pallas kernels, forward(): pl.pallas_call(forward_kernel, name='forward', out_shape=[jax.ShapeDtypeS...  115 us
    dot_general x5, matrix products, product(): jnp.einsum('sij,sjc->sic', left, right, preferred_element_type=jnp.float32)  10.5 us

commit v1 on v0

--- a/solution.py
+++ b/solution.py
@@ -526,19 +526,11 @@
     )(cols, outw, down, hidden, ids, boxes, cotangent, vec)
 
 
-KEPT = ((8, 5, 9, 4, 0, 1), (3, 10, 11, 6, 7, 2))
-EARLY = (((0, 8), (0, 3)), ((1, 5), (1, 10)), ((2, 9), (2, 11)), ((3, 4), (3, 6)), (None, (4, 7)))
-LATE = (((4, 0), (5, 2)), ((5, 1), None))
+KEPT = ((8, 5, 9, 0, 1, 4), (10, 3, 11, 2, 6, 7))
+EARLY = (((0, 8), (0, 10), 0), ((1, 5), None, 0), (None, (1, 3), 0), ((2, 9), (2, 11), 8))
+LATE = (((3, 0), (3, 2), 0), ((4, 1), None, 0), ((5, 4), (4, 6), 0), (None, (5, 7), 0))
 UNIT_ORDER = (0, 2, 1, 3)
 RING = 3
-
-
-def pick(values, e):
-    out = values[0]
-    for at in range(1, len(values)):
-        if values[at] != values[at - 1]:
-            out = out + (values[at] - values[at - 1]) * lax.div(e + 8 - at, 8)
-    return out
 
 
 def attend_pair_back(t, q8, k, v, ctx_grad, k_t, stat, dq_t, dk, dv):
@@ -569,24 +561,11 @@
         self.z, self.core, self.x, self.y, self.d = place
         self.p = 2 * self.y + self.x
         self.chunk, self.per, self.lag = chunk, WIDE // chunk, lag
-        self.count = len(entries) * self.per
         self.entries, self.refs, self.ring = entries, refs, ring
-        self.steps = self.count + 6 * lag + 5
-
-    def where(self, m):
-        e, r = lax.div(m, self.per), lax.rem(m, self.per)
-        slots = [[(0, 0, -1) if item is None else (item[0], item[1], 1) for item in (pair[c] for pair in self.entries)] for c in range(2)]
-
-        def both(function):
-            a = pick([function(item) for item in slots[0]], e)
-            b = pick([function(item) for item in slots[1]], e)
-            return a + self.core * (b - a)
-
-        q = both(lambda item: item[0])
-        j = both(lambda item: item[1] // 4)
-        i = both(lambda item: item[1] % 2)
-        live = both(lambda item: item[2])
-        return q, j, i, r, live
+        self.steps = max(entry[2] for entry in entries) + self.per + 6 * lag
+        x, y = self.x, self.y
+        self.corner = [(x if j % 2 == 0 else 1 - x, y if j // 2 == 0 else 1 - y) for j in range(3)]
+        self.by_x, self.by_y = 2 - 4 * x, 4 - 8 * y
 
     def rows(self, r):
         return pl.ds(pl.multiple_of(r * self.chunk, self.chunk), self.chunk)
@@ -597,36 +576,17 @@
             device_id=device, device_id_type=MESH,
         )
 
-    def role(self, j, r):
-        jx, jy = lax.rem(j, 2), lax.div(j, 2)
-        rx = self.x + jx - 2 * self.x * jx
-        ry = self.y + jy - 2 * self.y * jy
-        odd = lax.rem(r, 2)
-        first = rx + odd - 2 * rx * odd
-        second = ry + odd - 2 * ry * odd
-        even_code = 3 - 3 * rx - ry + 2 * rx * ry
-        odd_code = 3 - 3 * ry - rx + 2 * rx * ry
-        return even_code + odd * (odd_code - even_code), odd
-
-    def along(self, pos, odd):
-        turn = odd if pos != 1 else 1 - odd
-        return (self.d + turn * (2 - 4 * self.x) + (1 - turn) * (4 - 8 * self.y), self.z)
-
-    def forward(self, q, r, pos, odd):
+
+    def forward(self, q, r, turn):
         R = self.refs
         at = self.rows(r)
-        return self.remote(R["mine"].at[q, at, :], R["land"].at[q, at, :], R["send"].at[q, r], R["recv"].at[q, r], self.along(pos, odd))
-
-    def landed(self, q, r):
-        R = self.refs
-        at = self.rows(r)
-        return self.remote(R["land"].at[q, at, :], R["land"].at[q, at, :], R["send"].at[q, r], R["recv"].at[q, r], (self.d, self.z))
+        device = (self.d + self.by_y + turn * (self.by_x - self.by_y), self.z)
+        return self.remote(R["mine"].at[q, at, :], R["land"].at[q, at, :], R["send"].at[q, r], R["recv"].at[q, r], device)
 
     def chained(self, i, r, way):
         R = self.refs
         at = self.rows(r)
-        ref = R["chain"].at[way, i, at, :]
-        return ref, R["chain_send"].at[way, i, r], R["chain_recv"].at[way, i, r]
+        return R["chain"].at[way, i, at, :], R["chain_send"].at[way, i, r], R["chain_recv"].at[way, i, r]
 
     def pass_on(self, source, i, r, way):
         ref, ssem, rsem = self.chained(i, r, way)
@@ -637,71 +597,69 @@
         return pltpu.make_async_copy(source, R["total"].at[i, self.rows(r), :], R["out"].at[i, r])
 
     def add_to_mine(self, q, r, ref):
-        at = self.rows(r)
         mine = self.refs["mine"]
-        mine[q, at, :] = (mine[q, at, :].astype(jnp.float32) + ref[...].astype(jnp.float32)).astype(jnp.bfloat16)
-
-    def guarded(self, m, function):
-        @pl.when((m >= 0) & (m < self.count))
-        def _():
-            q, j, i, r, live = self.where(m)
-
-            @pl.when(live > 0)
-            def _():
-                function(m, q, j, i, r)
-
-
-    def begin_pair(self, m, q, j, i, r):
+
+        def part(g):
+            at = pl.ds(pl.multiple_of(r * self.chunk + g * 32, 32), 32)
+            here = pl.ds(pl.multiple_of(g * 32, 32), 32)
+            mine[q, at, :] = (mine[q, at, :].astype(jnp.float32) + ref[here, :].astype(jnp.float32)).astype(jnp.bfloat16)
+
+        loop(self.chunk // 32, part)
+
+    def load(self, e, kind, q, r):
+        source = self.refs["sib" if kind == 0 else "land"]
+        return pltpu.make_async_copy(source.at[q, self.rows(r), :], self.ring.at[e, kind], self.refs["ring_sem"].at[e, kind])
+
+    def begin_pair(self, e, q, j, i, r):
         R = self.refs
         quarter = 256 // self.chunk
 
-        @pl.when(lax.rem(r, quarter) == 0)
+        def arrival(f):
+            at = pl.ds(pl.multiple_of(f * 256, 256), 256)
+            ref = R["sib"].at[q, at, :]
+            self.remote(ref, ref, R["give_send"].at[q, f], R["give_recv"].at[q, f], (self.d, self.z)).wait_recv()
+
+        if quarter == 1:
+            arrival(r)
+        else:
+
+            @pl.when(lax.rem(r, quarter) == 0)
+            def _():
+                arrival(lax.div(r, quarter))
+
+        self.load(e, 0, q, r).start()
+
+    def end_pair(self, e, q, j, i, r):
+        self.load(e, 0, q, r).wait()
+        self.add_to_mine(q, r, self.ring.at[e, 0])
+        odd = lax.rem(r, 2)
+        rx, ry = self.corner[j]
+
+        @pl.when((rx + ry == 1) & (rx + odd == 1))
         def _():
-            f = lax.div(r, quarter)
-            at = pl.ds(pl.multiple_of(f * 256, 256), 256)
-            self.remote(R["sib"].at[q, at, :], R["sib"].at[q, at, :], R["give_send"].at[q, f], R["give_recv"].at[q, f], (self.d, self.z)).wait_recv()
-
-        slot = lax.rem(m, 2)
-        pltpu.make_async_copy(R["sib"].at[q, self.rows(r), :], self.ring.at[0, slot], R["ring_sem"].at[0, slot]).start()
-
-    def end_pair(self, m, q, j, i, r):
-        R = self.refs
-        slot = lax.rem(m, 2)
-        pltpu.make_async_copy(R["sib"].at[q, self.rows(r), :], self.ring.at[0, slot], R["ring_sem"].at[0, slot]).wait()
-        self.add_to_mine(q, r, self.ring.at[0, slot])
-        pos, odd = self.role(j, r)
-
-        @pl.when(pos == 0)
-        def _():
-            self.forward(q, r, 0, odd).start()
-
-    def begin_path(self, step_pos):
-        def run(m, q, j, i, r):
-            pos, odd = self.role(j, r)
-            R = self.refs
-
-            @pl.when(pos == step_pos)
+            self.forward(q, r, odd).start()
+
+    def path(self, hop, begin):
+        def run(e, q, j, i, r):
+            odd = lax.rem(r, 2)
+            rx, ry = self.corner[j]
+            here = {1: rx + ry == 2, 2: (rx + ry == 1) & (rx == odd), 3: rx + ry == 0}[hop]
+
+            @pl.when(here)
             def _():
-                slot = lax.rem(m, 2)
-                self.landed(q, r).wait_recv()
-                pltpu.make_async_copy(R["land"].at[q, self.rows(r), :], self.ring.at[step_pos, slot], R["ring_sem"].at[step_pos, slot]).start()
-
-        return run
-
-    def end_path(self, step_pos):
-        def run(m, q, j, i, r):
-            pos, odd = self.role(j, r)
-            R = self.refs
-
-            @pl.when(pos == step_pos)
-            def _():
-                slot = lax.rem(m, 2)
-                pltpu.make_async_copy(R["land"].at[q, self.rows(r), :], self.ring.at[step_pos, slot], R["ring_sem"].at[step_pos, slot]).wait()
-                self.add_to_mine(q, r, self.ring.at[step_pos, slot])
-                if step_pos < 3:
-                    self.forward(q, r, step_pos, odd).start()
-                else:
-                    mine = R["mine"].at[q, self.rows(r), :]
+                copy = self.load(e, 1, q, r)
+                if begin:
+                    self.forward(q, r, odd).wait_recv()
+                    copy.start()
+                    return
+                copy.wait()
+                self.add_to_mine(q, r, self.ring.at[e, 1])
+                if hop == 1:
+                    self.forward(q, r, 1 - odd).start()
+                if hop == 2:
+                    self.forward(q, r, odd).start()
+                if hop == 3:
+                    mine = self.refs["mine"].at[q, self.rows(r), :]
 
                     @pl.when(self.z == 0)
                     def _():
@@ -718,78 +676,132 @@
         at = self.rows(r)
         ref, ssem, rsem = self.chained(i, r, way)
         self.remote(ref, ref, ssem, rsem, (self.d, self.z)).wait_recv()
-        came = ref[...].astype(jnp.float32)
-        mine = R["mine"]
-        ref[...] = (mine[q, at, :].astype(jnp.float32) + came).astype(jnp.bfloat16)
+        mine, chain = R["mine"], R["chain"]
+
+        def part(g):
+            piece = pl.ds(pl.multiple_of(r * self.chunk + g * 32, 32), 32)
+            came = chain[way, i, piece, :].astype(jnp.float32)
+            chain[way, i, piece, :] = (mine[q, piece, :].astype(jnp.float32) + came).astype(jnp.bfloat16)
+            if last:
+                other = chain[1 - way, i, piece, :].astype(jnp.float32)
+                mine[q, piece, :] = (other + came).astype(jnp.bfloat16)
+
+        loop(self.chunk // 32, part)
         self.pass_on(ref, i, r, way).start()
         if last:
-            other = R["chain"][1 - way, i, at, :].astype(jnp.float32)
-            mine[q, at, :] = (other + came).astype(jnp.bfloat16)
             self.total_out(mine.at[q, at, :], i, r).start()
 
     def links(self, last):
-        def run(m, q, j, i, r):
-            for z, way in ((1, 1 if last else 0), (2, 0 if last else 1)):
-
-                @pl.when((self.p == j) & (self.z == z))
-                def _(way=way):
-                    self.link(q, i, r, way, last)
+        def run(e, q, j, i, r):
+            @pl.when(self.p == j)
+            def _():
+                for z, way in ((1, 1 if last else 0), (2, 0 if last else 1)):
+
+                    @pl.when(self.z == z)
+                    def _(way=way):
+                        self.link(q, i, r, way, last)
 
         return run
 
-    def ends(self, m, q, j, i, r):
+    def ends(self, e, q, j, i, r):
         R = self.refs
         at = self.rows(r)
-        for z, way in ((0, 1), (3, 0)):
-
-            @pl.when((self.p == j) & (self.z == z))
-            def _(way=way):
-                ref, ssem, rsem = self.chained(i, r, way)
-                self.remote(ref, ref, ssem, rsem, (self.d, self.z)).wait_recv()
-                ref[...] = (R["mine"][q, at, :].astype(jnp.float32) + ref[...].astype(jnp.float32)).astype(jnp.bfloat16)
-                self.total_out(ref, i, r).start()
+
+        @pl.when(self.p == j)
+        def _():
+            for z, way in ((0, 1), (3, 0)):
+
+                @pl.when(self.z == z)
+                def _(way=way):
+                    ref, ssem, rsem = self.chained(i, r, way)
+                    self.remote(ref, ref, ssem, rsem, (self.d, self.z)).wait_recv()
+                    mine, chain = R["mine"], R["chain"]
+
+                    def part(g):
+                        piece = pl.ds(pl.multiple_of(r * self.chunk + g * 32, 32), 32)
+                        chain[way, i, piece, :] = (
+                            mine[q, piece, :].astype(jnp.float32) + chain[way, i, piece, :].astype(jnp.float32)
+                        ).astype(jnp.bfloat16)
+
+                    loop(self.chunk // 32, part)
+                    self.total_out(ref, i, r).start()
+
+    def each(self, function):
+        for e, entry in enumerate(self.entries):
+            here = [item for item in entry[:2] if item is not None]
+            if len(here) == 2:
+                (q, slot), (q_other, slot_other) = here
+                assert slot // 4 == slot_other // 4
+                if q != q_other:
+                    q = q + self.core * (q_other - q)
+                i = slot % 2
+                if i != slot_other % 2:
+                    i = i + self.core * (slot_other % 2 - i)
+                function(e, entry[2], q, slot // 4, i)
+            else:
+                only = 0 if entry[1] is None else 1
+
+                @pl.when(self.core == only)
+                def _(e=e, entry=entry, item=here[0]):
+                    function(e, entry[2], item[0], item[1] // 4, item[1] % 2)
 
     def step(self, n):
         L = self.lag
-        parts = [
-            (0, self.begin_pair),
-            (1, self.end_pair),
-            (1 + L, self.begin_path(1)),
-            (2 + L, self.end_path(1)),
-            (2 + 2 * L, self.begin_path(2)),
-            (3 + 2 * L, self.end_path(2)),
-            (3 + 3 * L, self.begin_path(3)),
-            (4 + 3 * L, self.end_path(3)),
-            (4 + 4 * L, self.links(False)),
-            (4 + 5 * L, self.links(True)),
-            (4 + 6 * L, self.ends),
-        ]
-        for lag, part in reversed(parts):
-            self.guarded(n - lag, part)
-
-    def finish(self, m):
-        def run(m, q, j, i, r):
-            pos, odd = self.role(j, r)
-
-            @pl.when(pos < 3)
-            def _():
-                self.forward(q, r, 0, odd).wait_send()
-
-            mine = self.refs["mine"].at[q, self.rows(r), :]
-
-            @pl.when((pos == 3) & (self.z < 3))
-            def _():
-                self.pass_on(mine, i, r, 0).wait_send()
-
-            @pl.when((pos == 3) & (self.z > 0))
-            def _():
-                self.pass_on(mine, i, r, 1).wait_send()
-
-            @pl.when(pos == 3)
-            def _():
-                self.total_out(mine, i, r).wait()
-
-        self.guarded(m, run)
+        begins = ((0, self.begin_pair), (L, self.path(1, True)), (2 * L, self.path(2, True)), (3 * L, self.path(3, True)))
+        ends = (
+            (6 * L, self.ends),
+            (5 * L, self.links(True)),
+            (4 * L, self.links(False)),
+            (3 * L, self.path(3, False)),
+            (2 * L, self.path(2, False)),
+            (L, self.path(1, False)),
+            (0, self.end_pair),
+        )
+
+        def visit(parts):
+            def entry_parts(e, start, q, j, i):
+                m = n - start
+
+                @pl.when((m >= 0) & (m < self.per + 6 * L))
+                def _():
+                    for lag, part in parts:
+                        r = m - lag
+
+                        @pl.when((r >= 0) & (r < self.per))
+                        def _(r=r, part=part):
+                            part(e, q, j, i, r)
+
+            self.each(entry_parts)
+
+        visit(begins)
+        visit(ends)
+
+    def finish(self):
+        def chunk(e, start, q, j, i):
+            rx, ry = self.corner[j]
+
+            def body(r):
+                @pl.when(rx + ry > 0)
+                def _():
+                    self.forward(q, r, 0).wait_send()
+
+                mine = self.refs["mine"].at[q, self.rows(r), :]
+
+                @pl.when((rx + ry == 0) & (self.z < 3))
+                def _():
+                    self.pass_on(mine, i, r, 0).wait_send()
+
+                @pl.when((rx + ry == 0) & (self.z > 0))
+                def _():
+                    self.pass_on(mine, i, r, 1).wait_send()
+
+                @pl.when(rx + ry == 0)
+                def _():
+                    self.total_out(mine, i, r).wait()
+
+            loop(self.per, body)
+
+        self.each(chunk)
 
 
 def backward_kernel(
@@ -814,11 +826,12 @@
         shared, send=send_b, recv=recv_b, chain_send=chain_send_b, chain_recv=chain_recv_b, out=out_b, ring_sem=ring_sem_b,
     ), ring_b, place)
 
-    two_low, act_ring, up_grad = pb.at[0], (pb.at[1], pb.at[2]), pb.at[3]
+    two_low, act_ring = pb.at[0], (pb.at[1], pb.at[2])
+    up_grads = {0: pb.at[3], 2: pb.at[3], 1: pb.at[7], 3: pb.at[8]}
     k, q8, v = pb.at[4], pb.at[5], pb.at[6]
-    one_low, ctx, ctx_grad, dq, dk, dv = pb.at[0], pb.at[1], pb.at[2], pb.at[0], pb.at[1], pb.at[3]
+    one_low, ctx, ctx_grad, dq, dk, dv = pb.at[0], pb.at[1], pb.at[2], pb.at[0], pb.at[9], pb.at[3]
     two_t, mid_t, k_t = pt.at[0], pt.at[1], pt.at[2]
-    one_t, x_t, dq_t = pt.at[0], pt.at[1], pt.at[0]
+    one_t, x_t, dq_t = pt.at[0], pt.at[3], pt.at[4]
     two, back, slope_ring = pf.at[0], pf.at[1], (pf.at[2], pf.at[3])
     one, hat = pf.at[0], pf.at[2]
     uses = [slot for u in UNIT_ORDER for slot in (8 + u, 3 + u)] + [7, 0, 1, 2]
@@ -849,42 +862,31 @@
     slope_load(1).start()
     act_load(1).start()
     for name, source, dest in (
-        ("inv", inv_in, inv), ("k", k_in, k), ("q", q_in, q8), ("v", v_in, v), ("kt", kt_in, k_t), ("stat", stat_in, stat),
+        ("inv", inv_in, inv), ("k", k_in, k), ("q", q_in, q8), ("v", v_in, v), ("kt", kt_in, k_t), ("stat", stat_in, stat), ("x", x_in, x_t),
     ):
         fetch(name, source, dest)
     meet(z, near, (z_two,))
 
-    counter = {"early": 0, "late": 0, "whole": 0}
+    counter = {"early": 0}
     produced = set()
 
-    def run(count, body, per=0, every=1, stream=early, name="early"):
-        base = counter[name]
-        total_steps = (count // every) * per
+    def run(count, body, at=()):
+        base = counter["early"]
+        for one_entry in EARLY:
+            if at and one_entry[2] < base + len(at):
+                assert all(item is None or item[1] in produced for item in one_entry[:2])
 
         def one_turn(i):
             body(i)
-            if per:
-                if every == 1:
-                    for s in range(per):
-                        stream.step(base + i * per + s)
-                else:
-
-                    @pl.when(lax.rem(i, every) == every - 1)
-                    def _():
-                        for s in range(per):
-                            stream.step(base + lax.div(i, every) * per + s)
-
-        if per:
-            have = 0
-            for pair in stream.entries:
-                if all(item is None or item[1] in produced for item in pair):
-                    have += 1
-                else:
-                    break
-            limit = stream.steps if have == len(stream.entries) else have * stream.per
-            assert base + total_steps <= limit, (name, base, total_steps, limit)
+            if at:
+                first, stride = at[0], (at[1] - at[0] if len(at) > 1 else count)
+
+                @pl.when((i >= first) & (lax.rem(i - first + stride, stride) == 0))
+                def _():
+                    early.step(base + lax.div(i - first, stride))
+
         loop(count, one_turn)
-        counter[name] = base + total_steps
+        counter["early"] += len(at)
 
     def use(n):
         weight(n).wait()
@@ -904,7 +906,7 @@
             recv_sem=give_recv.at[q, f], device_id=near["c"], device_id_type=MESH,
         )
 
-    def block(slot, left_t, right, **steps):
+    def block(slot, left_t, right, at=()):
         owner = (slot // 2) % 2
         giver = 1 - owner
         q = KEPT[owner].index(slot)
@@ -927,7 +929,7 @@
             def _():
                 stage[n % 2, :, columns(i)] = value
 
-        run(WIDE // 256, tile, **steps)
+        run(WIDE // 256, tile, at)
 
         @pl.when(core == giver)
         def _():
@@ -963,19 +965,19 @@
         weights = use(2 * n)
         slope_load(n).wait()
         act_load(n).wait()
-        slope = slope_ring[n % 2]
+        slope, up_grad = slope_ring[n % 2], up_grads[u]
 
         def tile(i):
             rows = columns(i)
             grad = dot_nt(two_low[...], weights[rows, :]) * slope[:, rows]
             up_grad[:, rows] = grad.astype(jnp.bfloat16)
 
-        run(WIDE // 256, tile, **pace[0])
+        run(WIDE // 256, tile, pace[0])
         done(2 * n)
         if n == 2:
             fetch("hat", hat_in, hat)
         token_sum(8 + u, up_grad)
-        block(8 + u, two_t, act_ring[n % 2], **pace[1])
+        block(8 + u, two_t, act_ring[n % 2], pace[1])
         if n == 2:
             fetch("ctx", ctx_in, ctx)
         weights = use(2 * n + 1)
@@ -985,13 +987,13 @@
             value = dot_nt(up_grad[...], weights[at, :])
             back[:, at] = two[:, at] + value if n == 0 else back[:, at] + value
 
-        run(WIDE // 256, tile_back, **pace[2])
+        run(WIDE // 256, tile_back, pace[2])
         done(2 * n + 1)
-        block(3 + u, mid_t, up_grad, **pace[3])
+        if n < 2:
+            block(3 + u, mid_t, up_grad, pace[3])
         if n + 2 < 4:
             slope_load(n + 2).start()
             act_load(n + 2).start()
-    fetch("x", x_in, x_t)
     for name in ("hat", "inv"):
         loads[name].wait()
     sums[0:1, :] = jnp.zeros((1, WIDE), jnp.float32)
@@ -1008,7 +1010,7 @@
         sums[2:3, :] += jnp.sum(grad * normed, 0, keepdims=True)
         sums[3:4, :] += jnp.sum(grad, 0, keepdims=True)
 
-    run(TOKENS // SLICE, rows, **PACE[4])
+    run(TOKENS // SLICE, rows, PACE[4])
     transpose_into(one_t, one_low)
     weights = use(8)
 
@@ -1016,18 +1018,20 @@
         at = columns(i)
         ctx_grad[:, at] = dot_nt(one_low[...], weights[at, :]).astype(jnp.bfloat16)
 
-    run(WIDE // 256, tile_ctx, **PACE[5])
+    run(WIDE // 256, tile_ctx, PACE[5])
     done(8)
-    loads["ctx"].wait()
-    block(7, one_t, ctx, **PACE[6])
     for name in ("k", "q", "v", "kt", "stat"):
         loads[name].wait()
-    run(H // 2, lambda t: attend_pair_back(t, q8, k, v, ctx_grad, k_t, stat, dq_t, dk, dv), **PACE[7])
+    run(H // 2, lambda t: attend_pair_back(t, q8, k, v, ctx_grad, k_t, stat, dq_t, dk, dv), PACE[7])
     transpose_back(dq, dq_t)
     loads["x"].wait()
-    block(0, x_t, dq, **PACE[8])
-    block(2, x_t, dv, **PACE[8])
-    block(1, x_t, dk, **PACE[8])
+    block(0, x_t, dq, PACE[8])
+    block(2, x_t, dv)
+    block(1, x_t, dk)
+    block(4, mid_t, up_grads[1], PACE[8])
+    block(6, mid_t, up_grads[3])
+    loads["ctx"].wait()
+    block(7, one_t, ctx, PACE[8])
 
     def vec_hop(h):
         device = (near["c"], near["x"], near["y"], z_one, z_two)[h]
@@ -1042,20 +1046,30 @@
     hop = 0
     tail = {"early": counter["early"], "late": 0}
 
-    def both(count, rate, body=None):
+    def both(count, body=None, hops=False):
         base_late, base_early = tail["late"], tail["early"]
 
         def turn(i):
             if body is not None:
                 body(i)
-
-            for s in range(rate):
-                early.step(base_early + i * rate + s)
             late.step(base_late + i)
+            if hops:
+                for h in range(5):
+
+                    @pl.when(i == 1 + 2 * h)
+                    def _(h=h):
+                        vec_hop(h).wait()
+                        sums[...] = sums[...] + vec_in[h]
+                        if h < 4:
+                            vec_hop(h + 1).start()
+
+            @pl.when(lax.rem(i, LATE_TURNS) == LATE_TURNS - 1)
+            def _():
+                early.step(base_early + lax.div(i, LATE_TURNS))
 
         loop(count, turn)
         tail["late"] += count
-        tail["early"] += count * rate
+        tail["early"] += count // LATE_TURNS
 
     for kk, grad in ((0, dq), (1, dk), (2, dv)):
         weights = use(9 + kk)
@@ -1064,19 +1078,11 @@
             at = columns(i)
             one[:, at] = one[:, at] + dot_nt(grad[...], weights[at, :])
 
-        both(WIDE // 256, EARLY_RATE, tile_in)
+        both(WIDE // 256, tile_in)
     out = pltpu.make_async_copy(one, input_out, osem.at[0])
     out.start()
-    for h in range(5):
-        vec_hop(h).wait()
-        sums[...] = sums[...] + vec_in[h]
-        if h < 4:
-            vec_hop(h + 1).start()
-            both(4, EARLY_RATE)
-    left = max(0, -(-(early.steps - tail["early"]) // EARLY_RATE))
-    both(min(left, late.steps - tail["late"]), EARLY_RATE)
-    loop(late.steps - tail["late"], lambda i, base=tail["late"]: late.step(base + i))
-    assert tail["early"] >= early.steps
+    turns = max(late.steps - tail["late"], LATE_TURNS * (early.steps - tail["early"]))
+    both(-(-turns // LATE_TURNS) * LATE_TURNS, hops=True)
 
     for c in range(2):
 
@@ -1087,8 +1093,8 @@
                 for f in range(4):
                     give(given[c][n - back_by], c, n - back_by, f).wait_send()
 
-    loop(early.count, early.finish)
-    loop(late.count, late.finish)
+    early.finish()
+    late.finish()
     out.wait()
 
     @pl.when(p == 3)
@@ -1097,21 +1103,19 @@
 
 
 CHUNK_EARLY, CHUNK_LATE = 128, 64
-LAG_EARLY, LAG_LATE = 2, 3
-EARLY_RATE = 1
-NO = {}
-SLOW = {"per": 1, "every": 2}
-ONE = {"per": 1}
+LAG_EARLY, LAG_LATE = 2, 2
+LATE_TURNS = 1
+NO = ()
 PACE = (
     (NO, NO, NO, NO),
-    (SLOW, SLOW, SLOW, SLOW),
-    (SLOW, SLOW, SLOW, SLOW),
-    (NO, NO, SLOW, SLOW),
-    {"per": 1, "every": 4},
-    SLOW,
-    SLOW,
-    {"per": 1, "every": 2},
-    SLOW,
+    (NO, NO, NO, NO),
+    (NO, (3,), NO, NO),
+    ((3,), NO, (3,), NO),
+    NO,
+    (3,),
+    (3,),
+    (1, 3, 5, 7),
+    (3,),
 )
 
 
@@ -1123,8 +1127,8 @@
     page = (TOKENS, WIDE)
     many_a, many_b = WIDE // CHUNK_EARLY, WIDE // CHUNK_LATE
 
-    def stream_sems(many):
-        return [dma((6, many)), dma((6, many)), dma((2, 2, many)), dma((2, 2, many)), dma((2, many)), dma((4, 2))]
+    def stream_sems(many, entries):
+        return [dma((6, many)), dma((6, many)), dma((2, 2, many)), dma((2, 2, many)), dma((2, many)), dma((entries, 2))]
 
     return pl.pallas_call(
         backward_kernel,
@@ -1140,21 +1144,21 @@
         out_specs=[anywhere, anywhere, vmem, anywhere, anywhere],
         scratch_shapes=[
             pltpu.VMEM((RING, WIDE, WIDE), low),
-            pltpu.VMEM((7,) + page, low),
-            pltpu.VMEM((3, WIDE, TOKENS), low),
+            pltpu.VMEM((10,) + page, low),
+            pltpu.VMEM((5, WIDE, TOKENS), low),
             pltpu.VMEM((4,) + page, wide),
             pltpu.VMEM((H, 1, TOKENS), wide),
             pltpu.VMEM((TOKENS, 128), wide),
             pltpu.VMEM((2, WIDE, WIDE), low),
             pltpu.VMEM((6, WIDE, WIDE), low),
             pltpu.VMEM((2, 2, WIDE, WIDE), low),
-            pltpu.VMEM((4, 2, CHUNK_EARLY, WIDE), low),
-            pltpu.VMEM((4, 2, CHUNK_LATE, WIDE), low),
+            pltpu.VMEM((len(EARLY), 2, CHUNK_EARLY, WIDE), low),
+            pltpu.VMEM((len(LATE), 2, CHUNK_LATE, WIDE), low),
             pltpu.VMEM((5, 16, WIDE), wide),
             dma((RING,)), dma((2,)), dma((2,)), dma((12,)), dma((2,)),
             dma((6, 4)), dma((6, 4)),
-            *stream_sems(many_a),
-            *stream_sems(many_b),
+            *stream_sems(many_a, len(EARLY)),
+            *stream_sems(many_b, len(LATE)),
             dma((5,)), dma((5,)),
         ],
         compiler_params=pltpu.CompilerParams(

time: 442 us -> 385 us (0.87)
  Pallas kernels: 405 us -> 347 us
    pallas_call x1, Pallas kernels: 290 us -> 232 us  [backward(): pl.pallas_call(backward_kernel, name='backward', out_shape=[jax.ShapeDtyp...]
where the time goes in v1:
time: 385 us; the launch traced here: 378 us
  Pallas kernels  347 us (90%)
  matrix products  18.4 us (5%)
  local copies, waits for them, and re-layouts  6.93 us (2%)
  other arithmetic  4.18 us (1%)
    pallas_call x1, Pallas kernels, backward(): pl.pallas_call(backward_kernel, name='backward', out_shape=[jax.ShapeDtyp...  232 us
    pallas_call x1, Pallas kernels, forward(): pl.pallas_call(forward_kernel, name='forward', out_shape=[jax.ShapeDtypeS...  115 us
    dot_general x5, matrix products, product(): jnp.einsum('sij,sjc->sic', left, right, preferred_element_type=jnp.float32)  10.5 us

profile of v1, /device:TPU:0, one launch (start us, length us, event | category | flops | bytes accessed | tf_op | source)
XLA Modules:
  0.0 377.7 jit_solution(7892900791354793086)
XLA Ops:
  0.6 1.4 copy.27
  2.0 115.1 %forward.1 = (bf16[12,1024,1024]{2,1,0:T(8,128)(2,1)}, f32[512,1024]{1,0:T(8,128)}, bf16[1024,512]{1,0:T(8,128)(2,1)}, bf16[512,1024]{1,0:T(8,128)(2,1)}, bf16[5...) custom-call(bf16[7,1024,256]{2,1,0:T(8,128)(2,1)} %cols.1, ...), custom_call_target="tpu_custom_call" | custom-call | tf_op jit(solution)/shard_map/forward/pallas_call | solution.py:485
  117.1 232.2 %backward.1 = (f32[512,1024]{1,0:T(8,128)}, bf16[2,1024,1024]{2,1,0:T(8,128)(2,1)}, f32[16,1024]{1,0:T(8,128)}, bf16[6,1024,1024]{2,1,0:T(8,128)(2,1)}, bf16[6,1024,1024]{2,1,0:T(8,128)(2,1)}) custom-call(bf16[12,1024,1024]{2,1,0:T(8,128)(2,1)} %get-tuple-element.32.full, bf16[1024,512]{1,0:T(8,128)(2,1)} %get-tuple-element.33.x_in, ...), custom_call_target="tpu_custom_call" | custom-call | tf_op jit(solution)/shard_map/backward/pallas_call | solution.py:1133
  349.3 0.0 copy-start.6
  349.3 2.9 dynamic-slice_convert_fusion
  352.1 0.0 copy-done.6
  352.1 5.3 %add_multiply_fusion.1 = f32[2,256,1024]{2,1,0:T(8,128)} fusion(f32[2,256,1024]{2,1,0:T(8,128)S(1)} %copy-done.6, bf16[2,1024,1024]{2,1,0:T(8,128)(2,1)} %get-tuple-element.48, s32[]{:T(128)S(6)} %select_n.8), kind=kOutput, calls=%fused_computation.8 | convolution fusion | flops 1074790400 | bytes 9437188 | tf_op jit(solution)/shard_map/sic,sjc->sij/dot_general | solution.py:1403
  357.4 2.7 add_multiply_fusion
  360.1 1.8 fusion.1
  361.9 0.0 slice-start.1
  361.9 1.8 bitcast_add_fusion
  363.8 0.4 slice-done.1
  364.2 1.3 fusion.11
  365.5 0.0 copy-start.2
  365.5 0.0 copy-start.3
  365.5 1.3 fusion.2
  366.9 0.3 copy-done.2
  367.1 0.6 copy-done.3
  367.8 4.2 %multiply_add_fusion = (f32[2,256,1024]{2,1,0:T(8,128)}, bf16[2,256,1024]{2,1,0:T(8,128)(2,1)}, f32[2,256,1024]{2,1,0:T(8,128)}) fusion(f32[2,256,1024]{2,1,0:T(8,128)S(1)} %copy-done.2, f32[2,256,1024]{2,1,0:T(8,128)S(1)} %copy-done.3, f32[2,1024,1024]{2,1,0:T(8,128)S(1)} %bitcast.19, f32[2,256,1024]{1,2,0:T(8,128)S(1)} %bitcast_add_fusion, ...), kind=kOutput, calls=%fused_computation.3 | convolution fusion | flops 1086849024 | bytes 24117248 | tf_op jit(solution)/shard_map/sij,sjc->sic/dot_general | solution.py:1415
  372.0 1.3 multiply_subtract_fusion.1
  373.3 0.5 slice_bitcast_fusion
  373.8 1.3 copy.42
  375.1 1.0 copy-done.5
  376.2 1.3 copy.43
  (16 shorter events, 0.0 us)
Async XLA Ops:
  349.3 2.9 copy-start.6
  352.1 5.3 %copy-start = (bf16[2,1024,1024]{2,1,0:T(8,128)(2,1)S(1)}, bf16[2,1024,1024]{2,1,0:T(8,128)(2,1)}, u32[]{:S(2)}) copy-start(bf16[2,1024,1024]{2,1,0:T(8,128)(2,1)} %get-tuple-element.48) | copy-start | bytes 12582916
  352.1 5.3 %copy-start.7 = (f32[2,256,1024]{2,1,0:T(8,128)S(1)}, f32[2,256,1024]{2,1,0:T(8,128)}, u32[]{:S(2)}) copy-start(f32[2,256,1024]{2,1,0:T(8,128)} %param.25) | copy-start | bytes 6291460
  357.4 2.7 copy-start.1
  360.1 3.7 slice-start
  361.9 2.3 slice-start.1
  365.5 1.6 copy-start.2
  365.5 2.2 copy-start.3
  367.7 4.2 %copy-start.8 = (f32[128,12]{0,1:T(8,128)S(1)}, f32[128,12]{0,1:T(8,128)}, u32[]{:S(2)}) copy-start(f32[128,12]{0,1:T(8,128)} %param.23) | copy-start | bytes 18436
  367.8 6.1 %copy-start.4 = (f32[512,1024]{1,0:T(8,128)S(1)}, f32[512,1024]{1,0:T(8,128)}, u32[]{:S(2)}) copy-start(f32[512,1024]{1,0:T(8,128)} %get-tuple-element.31) | copy-start | bytes 6291460
  373.3 1.8 copy-start.9
  373.8 2.3 copy-start.5
